TPU v7x, 32 devices: a whole 2x2x4 slice. The times are simulated.
32 devices in a mesh: row: 4 (over z), col: 8 (over y, x, core).
Axes of the slice: x: 2, y: 2, z: 4, core: 2. Of those that a mesh axis runs over, the one named last changes fastest.
Arguments:
- velocity: bfloat16 [3, 4, 4128, 4096], P(None, None, 'row', 'col'), may hold values from -6 to 6
- rhs_prev: bfloat16 [3, 4, 4128, 4096], P(None, None, 'row', 'col'), may hold values from -12 to 12
- row_counts: int32 [4], replicated, may hold values from 1016 to 1032, as said below
- x_scale: float32 [4096], P('col'), may hold values from 0.5 to 2
- x_curv: float32 [4096], P('col'), may hold values from -3 to 3
- y_scale: float32 [4128], P('row'), may hold values from 0.5 to 12
- y_curv: float32 [4128], P('row'), may hold values from -3 to 3
- x_local: bfloat16 [516, 2, 512], replicated, may hold values from -0.25 to 0.25
- x_coupling: float32 [2, 16, 16], replicated, may hold values from -1.5 to 1.5
- x_basis: float32 [2, 2, 512], replicated, may hold values from -3 to 3
- y_local: bfloat16 [4144, 2, 1032], P('row'), may hold values from -0.1875 to 0.1875
- y_coupling: float32 [2, 8, 8], replicated, may hold values from -2 to 2
- y_basis: float32 [4, 2, 2, 1032], P('row'), may hold values from -3 to 3
Outputs:
- rhs: bfloat16 [3, 4, 4128, 4096], P(None, None, 'row', 'col')
- increment: bfloat16 [3, 4, 4128, 4096], P(None, None, 'row', 'col')
Inputs may be any that keep to these rules, and one draw needn't show every extreme that they name: `row_counts`: the counts sum to 4097; each is at least 2, and the largest is exactly 1032.
All inputs are finite; a program needn't handle non-finite values.
Results may differ from a plain program's by a relative error of at most 0.0055.
Values may be sent and summed in bfloat16 or wider, within the bound.
A program may use at most 320 MiB of HBM per device.

v0:
```python
import jax
import jax.numpy as jnp
from jax import lax
from jax.sharding import PartitionSpec as P

viscosity = 0.1
cfl_target = 1.5
gamma_coef = 5.0 / 12.0
zeta_coef = -17.0 / 60.0


def padded_2(block, sides, width, periodic):
    for axis, dim in sides:
        count = lax.axis_size(axis)
        forward = [(i, i + 1) for i in range(count - 1)]
        if periodic:
            forward.append((count - 1, 0))
        backward = [(target, source) for source, target in forward]
        low = lax.ppermute(
            lax.slice_in_dim(block, block.shape[dim] - width, None, axis=dim), axis, forward
        )
        high = lax.ppermute(lax.slice_in_dim(block, 0, width, axis=dim), axis, backward)
        block = jnp.concatenate([low, block, high], axis=dim)
    return block


def shards(
    velocity,
    rhs_prev,
    row_counts,
    x_scale,
    x_curv,
    y_scale,
    y_curv,
    x_local,
    x_coupling,
    x_basis,
    y_local,
    y_coupling,
    y_basis,
):
    n_comp, n_plane, y_rows, x_width = velocity.shape
    col_pos = lax.axis_index("col")
    row_pos = lax.axis_index("row")
    own_count = row_counts[row_pos]
    slot_ids = jnp.arange(y_rows, dtype=jnp.int32)
    valid_rows = slot_ids < own_count
    speeds = (
        jnp.abs(velocity[0].astype(jnp.float32)) * x_scale
        + jnp.abs(velocity[1].astype(jnp.float32)) * y_scale[:, None]
    )
    local_top = jnp.max(jnp.where(valid_rows[:, None], speeds, jnp.float32(0.0)))
    speed_top = lax.pmax(local_top, ("row", "col"))
    time_step = cfl_target / (speed_top + 1e-06)
    line_rows = velocity.reshape(n_comp * n_plane * y_rows, x_width)
    line_count = line_rows.shape[0]
    padded = padded_2(line_rows, (("col", 1),), 2, True)
    local_x = jnp.dot(
        padded, x_local.reshape(x_width + 4, 2 * x_width), preferred_element_type=jnp.float32
    )
    ends_x = jnp.stack(
        [
            jnp.stack([local_x[:, 0], local_x[:, x_width]]),
            jnp.stack([local_x[:, x_width - 1], local_x[:, 2 * x_width - 1]]),
        ]
    )
    every_end = lax.all_gather(ends_x.astype(jnp.bfloat16), "col", axis=0, tiled=True).astype(
        ends_x.dtype
    )
    own_rows = lax.dynamic_slice_in_dim(x_coupling, 2 * col_pos, 2, 1)
    solved_x = jnp.einsum("kim,mkl->ikl", own_rows, every_end, precision=lax.Precision.HIGHEST)
    result_x = (
        local_x.reshape(line_count, 2, x_width)
        + jnp.transpose(solved_x[0])[:, :, None] * x_basis[:, 0, :]
        + jnp.transpose(solved_x[1])[:, :, None] * x_basis[:, 1, :]
    )
    first_x = result_x[:, 0].reshape(n_comp, n_plane, y_rows, x_width)
    second_x = result_x[:, 1].reshape(n_comp, n_plane, y_rows, x_width)
    columns = n_comp * n_plane * x_width
    stacked = jnp.transpose(velocity, (2, 0, 1, 3)).reshape(y_rows, columns)
    stacked = jnp.where(valid_rows[:, None], stacked, jnp.zeros((), jnp.bfloat16))
    edge_rows = jnp.concatenate(
        [stacked[0:2], lax.dynamic_slice_in_dim(stacked, own_count - 2, 2, 0)], axis=0
    )
    rimmed = padded_2(edge_rows, (("row", 0),), 2, False)
    extended = jnp.concatenate([rimmed[0:2], stacked, rimmed[6:8]], axis=0)
    local_y = lax.dot_general(
        y_local.reshape(y_rows + 4, 2 * y_rows),
        extended,
        (((0,), (0,)), ((), ())),
        preferred_element_type=jnp.float32,
    )
    local_y = local_y.reshape(2, y_rows, columns)
    first_rows = local_y[:, 0, :]
    last_rows = lax.dynamic_index_in_dim(local_y, own_count - 1, 1, keepdims=False)
    ends_y = jnp.stack([first_rows, last_rows])
    every_end = lax.all_gather(ends_y, "row", axis=0, tiled=True)
    own_rows = lax.dynamic_slice_in_dim(y_coupling, 2 * row_pos, 2, 1)
    solved_y = jnp.einsum("kim,mkl->ikl", own_rows, every_end, precision=lax.Precision.HIGHEST)
    basis_y = y_basis[0]
    result_y = (
        local_y
        + solved_y[0][:, None, :] * basis_y[:, 0, :, None]
        + solved_y[1][:, None, :] * basis_y[:, 1, :, None]
    )
    first_y = jnp.transpose(result_y[0].reshape(y_rows, n_comp, n_plane, x_width), (1, 2, 0, 3))
    second_y = jnp.transpose(result_y[1].reshape(y_rows, n_comp, n_plane, x_width), (1, 2, 0, 3))
    scale_y = y_scale[:, None]
    curve_y = y_curv[:, None]
    velocity_f = velocity.astype(jnp.float32)
    grad_x = x_scale * first_x
    grad_y = scale_y * first_y
    laplacian = (
        x_scale * x_scale * second_x
        + x_curv * first_x
        + scale_y * scale_y * second_y
        + curve_y * first_y
    )
    rhs_full = -(velocity_f[0:1] * grad_x + velocity_f[1:2] * grad_y) + viscosity * laplacian
    live_mask = valid_rows[None, None, :, None]
    rhs_full = jnp.where(live_mask, rhs_full, jnp.float32(0.0))
    change = time_step * (gamma_coef * rhs_full + zeta_coef * rhs_prev.astype(jnp.float32))
    change = jnp.where(live_mask, change, jnp.float32(0.0))
    return (rhs_full.astype(jnp.bfloat16), change.astype(jnp.bfloat16))


def solution(mesh):
    placed = (
        P(None, None, "row", "col"),
        P(None, None, "row", "col"),
        P(),
        P("col"),
        P("col"),
        P("row"),
        P("row"),
        P(),
        P(),
        P(),
        P("row", None, None),
        P(),
        P("row", None, None, None),
    )
    return jax.shard_map(
        shards,
        mesh=mesh,
        in_specs=placed,
        out_specs=(P(None, None, "row", "col"), P(None, None, "row", "col")),
        check_vma=False,
    )
```

profile of v0, /device:TPU:1, one launch (start us, length us, event | category | flops | bytes accessed | tf_op | source)
XLA Modules:
  0.0 600.5 jit_solution(1185752626311364632)
XLA Ops:
  0.6 4.6 fusion.26
  5.2 3.9 copy.50
  17.9 34.1 %copy.56 = bf16[1032,3,4,512]{3,2,1,0:T(4,128)(2,1)} copy(bf16[1032,3,4,512]{3,0,2,1:T(8,128)(2,1)} %bitcast.97) | data formatting | bytes 25362432 | tf_op jit(solution)/shard_map/transpose | solution.py:80
  52.0 23.9 %reshape.56 = bf16[1032,6144]{1,0:T(8,128)(2,1)} reshape(bf16[1032,3,4,512]{3,2,1,0:T(4,128)(2,1)} %copy.56) | data formatting | bytes 25362432 | tf_op jit(solution)/shard_map/reshape | solution.py:80
  75.9 8.7 %broadcast_select_fusion = bf16[1032,6144]{1,0:T(8,128)(2,1)S(1)} fusion(bf16[1032,6144]{1,0:T(8,128)(2,1)} %reshape.56, pred[1032]{0:T(1024)(128)(4,1)S(1)} %iota_compare_fusion), kind=kLoop, calls=%fused_computation.20 | loop fusion | flops 6340608 | bytes 25363464 | tf_op jit(solution)/shard_map/jit(_where)/select_n | solution.py:81
  84.6 4.8 copy-done.1
  94.0 9.4 %convert_element_type.22 = f32[3,4,1032,512]{3,2,1,0:T(8,128)} convert(bf16[3,4,1032,512]{3,2,1,0:T(8,128)(2,1)S(1)} %bitcast.100) | non-fusion elementwise | flops 6340608 | bytes 38043648 | tf_op jit(solution)/shard_map/convert_element_type | solution.py:110
  103.5 11.2 %slice_bitcast_fusion.1 = (f32[4,1032,512]{2,1,0:T(8,128)}, f32[4,1032,512]{2,1,0:T(8,128)}) fusion(f32[3,4,1032,512]{3,2,1,0:T(8,128)} %convert_element_type.22), kind=kLoop, calls=%fused_computation.22 | loop fusion | bytes 33816576 | tf_op jit(solution)/shard_map/mul | solution.py:119
  114.7 3.4 fusion.14
  118.7 41.6 %pmax.7 = f32[]{:T(128)} all-reduce(f32[]{:T(128)} %fusion.14), channel_id=1, replica_groups=mesh['row'=4,'col'=8] {'row','col'}, use_global_device_ids=true, to_apply=%region_1.2 | all-reduce | flops 1 | bytes 8 | tf_op jit(solution)/shard_map/pmax | solution.py:53
  165.6 65.5 %concatenate.7 = bf16[1036,6144]{1,0:T(8,128)(2,1)} concatenate(bf16[2,6144]{1,0:T(2,128)(2,1)S(1)} %collective-permute-done.2, bf16[1032,6144]{1,0:T(8,128)(2,1)} %copy-done.1, bf16[2,6144]{1,0:T(2,128)(2,1)S(1)} %collective-permute-done.3), dimensions={0} | concatenate | bytes 25460736 | tf_op jit(solution)/shard_map/concatenate | solution.py:86
  231.1 40.1 %fusion.33 = f32[6144,2064]{0,1:T(8,128)} fusion(bf16[1036,6144]{1,0:T(8,128)(2,1)} %concatenate.7, bf16[1036,2064]{0,1:T(8,128)(2,1)} %bitcast.113), kind=kOutput, calls=%fused_computation.67 | convolution fusion | flops 26275479552 | bytes 67731840 | tf_op jit(solution)/shard_map/dot_general | solution.py:87
  272.5 12.7 %all_gather.7 = f32[8,2,6144]{2,1,0:T(2,128)S(1)} all-gather(f32[2,2,6144]{2,1,0:T(2,128)S(1)} %pad_maximum_fusion.1), channel_id=1, replica_groups=mesh['row'=4,'col'=8] {'row'}, dimensions={0}, use_global_device_ids=true | all-gather | bytes 491520 | tf_op jit(solution)/shard_map/all_gather | solution.py:97
  286.8 34.3 %multiply_add_fusion = f32[2,1032,6144]{2,1,0:T(8,128)} fusion(f32[2,1032,6144]{2,1,0:T(8,128)} %bitcast.104, f32[2,1032]{1,0:T(2,128)S(1)} %get-tuple-element.32, f32[2,6144]{1,0:T(2,128)S(1)} %bitcast.110, f32[2,1032]{1,0:T(2,128)S(1)} %get-tuple-element.33, f32[2,6144]{1,0:T(2,128)S(1)} %bitcast.111), kind=kLoop, calls=%fused_computation.2 | loop fusion | flops 50724864 | bytes 101564544 | tf_op jit(solution)/shard_map/add | solution.py:102
  321.1 32.1 %fusion.23 = (f32[1,1032,6144]{2,1,0:T(8,128)}, f32[1,1032,6144]{2,1,0:T(8,128)}) fusion(f32[2,1032,6144]{2,1,0:T(8,128)} %multiply_add_fusion), kind=kLoop, calls=%fused_computation.57 | loop fusion | bytes 101449728 | tf_op jit(solution)/shard_map/slice | solution.py:106
  353.2 29.3 %reshape_squeeze.13 = f32[1032,3,4,512]{3,2,1,0:T(4,128)} reshape(f32[1,1032,6144]{2,1,0:T(8,128)} %get-tuple-element.10) | data formatting | bytes 50724864 | tf_op jit(solution)/shard_map/reshape;squeeze | solution.py:106
  382.5 29.3 %reshape_squeeze.15 = f32[1032,3,4,512]{3,2,1,0:T(4,128)} reshape(f32[1,1032,6144]{2,1,0:T(8,128)} %get-tuple-element.11) | data formatting | bytes 50724864 | tf_op jit(solution)/shard_map/reshape;squeeze | solution.py:107
  415.0 3.5 copy.53
  418.5 34.6 %fusion.32 = (bf16[12384,1024]{1,0:T(8,128)(2,1)}, f32[12384,1024]{1,0:T(8,128)}) fusion(bf16[516,1024]{1,0:T(8,128)(2,1)} %bitcast.107, bf16[12384,2]{1,0:T(8,128)(2,1)} %copy.53, bf16[12384,512]{1,0:T(8,128)(2,1)} %bitcast.98, bf16[12384,2]{1,0:T(8,128)(2,1)S(1)} %copy.52), kind=kOutput, calls=%fused_computation.66 | convolution fusion | flops 13138036736 | bytes 89924352 | tf_op jit(solution)/shard_map/dot_general | solution.py:58
  453.1 10.6 %slice_reduce_fusion.3 = (bf16[12384]{0:T(1024)(128)(2,1)S(1)}, bf16[12384]{0:T(1024)(128)(2,1)S(1)}, bf16[12384]{0:T(1024)(128)(2,1)S(1)}, bf16[12384]{0:T(1024)(128)(2,1)S(1)}) fusion(bf16[12384,1024]{1,0:T(8,128)(2,1)} %get-tuple-element.30), kind=kLoop, calls=%fused_computation.32 | loop fusion | bytes 198144 | tf_op jit(solution)/shard_map/slice | solution.py:63
  464.3 15.2 %all_gather.6 = bf16[16,2,12384]{2,1,0:T(2,128)(2,1)S(1)} all-gather(bf16[2,2,12384]{2,1,0:T(2,128)(2,1)S(1)} %pad_maximum_fusion), channel_id=1, replica_groups=mesh['row'=4,'col'=8] {'col'}, dimensions={0}, use_global_device_ids=true | all-gather | bytes 891648 | tf_op jit(solution)/shard_map/all_gather | solution.py:67
  480.3 34.5 %fusion = f32[12384,2,512]{2,0,1:T(8,128)} fusion(f32[1548,2,8,512]{3,2,1,0:T(8,128)} %bitcast.105, f32[2,512]{1,0:T(2,128)S(1)} %copy-done.11, f32[12384,2]{0,1:T(2,128)S(1)} %bitcast.108, f32[2,512]{1,0:T(2,128)S(1)} %copy-done.12, f32[12384,2]{0,1:T(2,128)S(1)} %bitcast.109), kind=kLoop, calls=%fused_computation.1 | loop fusion | flops 50724864 | bytes 101656064 | tf_op jit(solution)/shard_map/add | solution.py:73
  514.8 32.2 %fusion.24 = (f32[12384,1,512]{2,0,1:T(8,128)}, f32[12384,1,512]{2,0,1:T(8,128)}) fusion(f32[12384,2,512]{2,0,1:T(8,128)} %fusion), kind=kLoop, calls=%fused_computation.58 | loop fusion | bytes 101449728 | tf_op jit(solution)/shard_map/slice | solution.py:78
  547.1 53.0 %select_convert_fusion = (bf16[3,4,1032,512]{3,2,1,0:T(8,128)(2,1)}, bf16[3,4,1032,512]{3,2,1,0:T(8,128)(2,1)}) fusion(bf16[3,4,1032,512]{3,2,1,0:T(8,128)(2,1)} %param.14, f32[]{:T(128)S(6)} %div.3, pred[1032]{0:T(1024)(128)(4,1)S(1)} %copy-done.6, f32[1032]{0:T(1024)S(1)} %copy-done.13, f32[1032,3,4,512]{3,2,1,0:T(4,128)} %reshape_squeeze.15, ...), kind=kLoop, calls=%fused_computation.12 | loop fusion | flops 152174592 | bytes 156421232 | tf_op jit(solution)/shard_map/convert_element_type | solution.py:124
  (80 shorter events, 23.0 us)
Async XLA Ops:
  0.6 478.9 %copy-start = (f32[2,16,16]{2,1,0:T(8,128)S(1)}, f32[2,16,16]{2,1,0:T(8,128)}, u32[]{:S(2)}) copy-start(f32[2,16,16]{2,1,0:T(8,128)} %param.21) | copy-start | bytes 6148
  9.1 402.7 %collective-permute-start = (bf16[12384,2]{0,1:T(2,128)(2,1)}, bf16[12384,2]{0,1:T(2,128)(2,1)}, u32[]{:S(2)}, u32[]{:S(2)}) collective-permute-start(bf16[12384,2]{0,1:T(2,128)(2,1)} %copy.50), channel_id=1, source_target_pairs={{0,1},{1,2},{2,3},{3,4},{4,5},{5,6},{6,7},{7,0},{8,9},{9,10},{10,1... | collective-permute-start | bytes 148616 | tf_op jit(solution)/shard_map/ppermute | solution.py:19
  14.6 400.4 %collective-permute-start.1 = (bf16[12384,2]{0,1:T(2,128)(2,1)}, bf16[12384,2]{0,1:T(2,128)(2,1)}, u32[]{:S(2)}, u32[]{:S(2)}) collective-permute-start(bf16[12384,2]{0,1:T(2,128)(2,1)} %copy.51), channel_id=1, source_target_pairs={{1,0},{2,1},{3,2},{4,3},{5,4},{6,5},{7,6},{0,7},{9,8},{10,9},{11,1... | collective-permute-start | bytes 148616 | tf_op jit(solution)/shard_map/ppermute | solution.py:22
  16.6 98.1 %copy-start.5 = (pred[1032]{0:T(1024)(128)(4,1)}, pred[1032]{0:T(1024)(128)(4,1)S(1)}, u32[]{:S(2)}) copy-start(pred[1032]{0:T(1024)(128)(4,1)S(1)} %iota_compare_fusion) | copy-start | bytes 3100
  75.9 18.1 %slice-start = ((s8[12681216]{0:T(1024)(128)(4,1)}), s8[98304]{0:T(1024)(128)(4,1)S(1)}, s32[]{:S(2)}) async-start(s8[12681216]{0:T(1024)(128)(4,1)} %bitcast.99), calls=%async_computation | async-start | bytes 196608
  75.9 18.1 %slice-start.1 = ((s8[12681216]{0:T(1024)(128)(4,1)}), s8[4194304]{0:T(1024)(128)(4,1)S(1)}, s32[]{:S(2)}) async-start(s8[12681216]{0:T(1024)(128)(4,1)} %bitcast.99), calls=%async_computation.1 | async-start | bytes 8388608
  75.9 18.1 %slice-start.2 = ((s8[12681216]{0:T(1024)(128)(4,1)}), s8[4194304]{0:T(1024)(128)(4,1)S(1)}, s32[]{:S(2)}) async-start(s8[12681216]{0:T(1024)(128)(4,1)} %bitcast.99), calls=%async_computation.2 | async-start | bytes 8388608
  75.9 18.2 %slice-start.3 = ((s8[12681216]{0:T(1024)(128)(4,1)}), s8[4194304]{0:T(1024)(128)(4,1)S(1)}, s32[]{:S(2)}) async-start(s8[12681216]{0:T(1024)(128)(4,1)} %bitcast.99), calls=%async_computation.3 | async-start | bytes 8388608
  89.4 14.0 %copy-start.15 = (f32[2,2,512]{2,1,0:T(2,128)S(1)}, f32[2,2,512]{2,1,0:T(2,128)}, u32[]{:S(2)}) copy-start(f32[2,2,512]{2,1,0:T(2,128)} %param.22) | copy-start | bytes 24580
  89.4 14.0 %copy-start.10 = (f32[1,2,2,1032]{3,2,1,0:T(2,128)S(1)}, f32[1,2,2,1032]{3,2,1,0:T(2,128)}, u32[]{:S(2)}) copy-start(f32[1,2,2,1032]{3,2,1,0:T(2,128)} %param.25) | copy-start | bytes 49540
  89.5 76.1 %collective-permute-start.2 = (bf16[2,6144]{1,0:T(2,128)(2,1)S(1)}, bf16[2,6144]{1,0:T(2,128)(2,1)S(1)}, u32[]{:S(2)}, u32[]{:S(2)}) collective-permute-start(bf16[2,6144]{1,0:T(2,128)(2,1)S(1)} %get-tuple-element.21), channel_id=1, source_target_pairs={{0,8},{8,16},{16,24},{1,9},{9,17},{17,25},{2,10},{10,18},{18,26},{... | collective-permute-start | bytes 73736 | tf_op jit(solution)/shard_map/ppermute | solution.py:19
  92.7 72.9 %collective-permute-start.3 = (bf16[2,6144]{1,0:T(2,128)(2,1)S(1)}, bf16[2,6144]{1,0:T(2,128)(2,1)S(1)}, u32[]{:S(2)}, u32[]{:S(2)}) collective-permute-start(bf16[2,6144]{1,0:T(2,128)(2,1)S(1)} %get-tuple-element.20), channel_id=1, source_target_pairs={{8,0},{16,8},{24,16},{9,1},{17,9},{25,17},{10,2},{18,10},{26,18},{... | collective-permute-start | bytes 73736 | tf_op jit(solution)/shard_map/ppermute | solution.py:22
  103.4 11.3 %copy-start.3 = (f32[1032]{0:T(1024)S(1)}, f32[1032]{0:T(1024)}, u32[]{:S(2)}) copy-start(f32[1032]{0:T(1024)} %param.18) | copy-start | bytes 12388
  103.4 11.3 %copy-start.8 = (f32[512]{0:T(512)S(1)}, f32[512]{0:T(512)}, u32[]{:S(2)}) copy-start(f32[512]{0:T(512)} %param.16) | copy-start | bytes 6148
  103.4 58.1 %copy-start.2 = (bf16[516,2,512]{2,1,0:T(2,128)(2,1)S(1)}, bf16[516,2,512]{2,1,0:T(2,128)(2,1)}, u32[]{:S(2)}) copy-start(bf16[516,2,512]{2,1,0:T(2,128)(2,1)} %param.20) | copy-start | bytes 3170308
  418.5 61.8 %copy-start.11 = (f32[2,512]{1,0:T(2,128)S(1)}, f32[2,512]{1,0:T(2,128)}, u32[]{:S(2)}) copy-start(f32[2,512]{1,0:T(2,128)} %get-tuple-element.36) | copy-start | bytes 12292
  418.5 61.8 %copy-start.12 = (f32[2,512]{1,0:T(2,128)S(1)}, f32[2,512]{1,0:T(2,128)}, u32[]{:S(2)}) copy-start(f32[2,512]{1,0:T(2,128)} %get-tuple-element.37) | copy-start | bytes 12292
  514.7 32.3 %copy-start.4 = (f32[1032]{0:T(1024)S(1)}, f32[1032]{0:T(1024)}, u32[]{:S(2)}) copy-start(f32[1032]{0:T(1024)} %param.18) | copy-start | bytes 12388
  514.7 32.3 %copy-start.6 = (pred[1032]{0:T(1024)(128)(4,1)S(1)}, pred[1032]{0:T(1024)(128)(4,1)}, u32[]{:S(2)}) copy-start(pred[1032]{0:T(1024)(128)(4,1)} %copy-done.5) | copy-start | bytes 3100
  514.7 32.3 %copy-start.7 = (f32[1032]{0:T(1024)S(1)}, f32[1032]{0:T(1024)}, u32[]{:S(2)}) copy-start(f32[1032]{0:T(1024)} %mul.230) | copy-start | bytes 12388
  514.7 32.3 %copy-start.9 = (f32[512]{0:T(512)S(1)}, f32[512]{0:T(512)}, u32[]{:S(2)}) copy-start(f32[512]{0:T(512)} %param.16) | copy-start | bytes 6148
  514.8 32.3 %copy-start.13 = (f32[1032]{0:T(1024)S(1)}, f32[1032]{0:T(1024)}, u32[]{:S(2)}) copy-start(f32[1032]{0:T(1024)} %param.19) | copy-start | bytes 12388
  514.8 32.3 %copy-start.14 = (f32[512]{0:T(512)S(1)}, f32[512]{0:T(512)}, u32[]{:S(2)}) copy-start(f32[512]{0:T(512)} %mul.225) | copy-start | bytes 6148
  514.8 32.3 %copy-start.16 = (f32[512]{0:T(512)S(1)}, f32[512]{0:T(512)}, u32[]{:S(2)}) copy-start(f32[512]{0:T(512)} %param.17) | copy-start | bytes 6148
  (1 other events, 4.8 us)
where the time goes:
time: 612 us; the launch traced here: 600 us
  local copies, waits for them, and re-layouts  297 us (49%)
  other arithmetic  145 us (24%)
  matrix products  76.6 us (13%)
  blocking collectives  69.6 us (11%)
  starting transfers between devices  7.09 us (1%)
    concatenate x1, local copies, waits for them, and re-layouts, shards(): extended = jnp.concatenate([rimmed[0:2], stacked, rimmed[6:8]], axis=0)  65.5 us
    convert_element_type x1, other arithmetic, shards(): return (rhs_full.astype(jnp.bfloat16), change.astype(jnp.bfloat16))  53 us
    pmax x1, blocking collectives, shards(): speed_top = lax.pmax(local_top, ('row', 'col'))  41.6 us
    dot_general x1, matrix products, shards(): lax.dot_general(y_local.reshape(y_rows + 4, 2 * y_rows), extended, (((0,)...  40.1 us
    dot_general x1, matrix products, shards(): jnp.dot(padded, x_local.reshape(x_width + 4, 2 * x_width), preferred_elem...  34.6 us
    add x1, other arithmetic, shards(): local_x.reshape(line_count, 2, x_width)  34.5 us
    add x1, other arithmetic, shards(): local_y + solved_y[0][:, None, :] * basis_y[:, 0, :, None]  34.3 us
    transpose x1, local copies, waits for them, and re-layouts, shards(): stacked = jnp.transpose(velocity, (2, 0, 1, 3)).reshape(y_rows, columns)  34.1 us
  transfers between devices with their start and end apart: 4, of which 0 were waited for; matrix products, arithmetic and copies ran while one was open for 56% of the time, Pallas kernels for 0%

commit v1 on v0

v1 whole, which is shorter than its diff:
```python
import functools
import jax
import jax.numpy as jnp
from jax import lax
from jax.experimental import pallas as pl
from jax.experimental.pallas import tpu as pltpu
from jax.sharding import PartitionSpec as P

viscosity = 0.1
cfl_target = 1.5
gamma_coef = 5.0 / 12.0
zeta_coef = -17.0 / 60.0
f32 = jnp.float32
bf16 = jnp.bfloat16


def dot(a, b, ca=1, cb=0):
    return lax.dot_general(a, b, (((ca,), (cb,)), ((), ())), preferred_element_type=f32)


def stats_kernel(vel, wx, wy, xs, ycol, xo, yo, top, xacc, yacc, peak):
    z = pl.program_id(0)
    speed = (
        jnp.abs(vel[0, 0].astype(f32)) * xs[...] + jnp.abs(vel[1, 0].astype(f32)) * ycol[:, 0:1]
    ) * ycol[:, 1:2]
    best = jnp.max(speed, axis=0, keepdims=True)
    for f in range(vel.shape[0]):
        block = vel[f, 0]
        px = dot(wx[0], block, 1, 1)
        py = dot(wy[0], block)

        @pl.when(z == 0)
        def _():
            xacc[f] = px
            yacc[f] = py

        @pl.when(z > 0)
        def _():
            xacc[f] = xacc[f] + px
            yacc[f] = yacc[f] + py

    @pl.when(z == 0)
    def _():
        peak[...] = best

    @pl.when(z > 0)
    def _():
        peak[...] = jnp.maximum(peak[...], best)

    @pl.when(z == pl.num_programs(0) - 1)
    def _():
        group = xo.shape[1] // vel.shape[0]
        for f in range(vel.shape[0]):
            for g in range(xo.shape[0]):
                xo[g, f * group : (f + 1) * group, :] = xacc[
                    f, g * group : (g + 1) * group, :
                ].astype(bf16)
            for g in range(yo.shape[0]):
                yo[g, f * group : (f + 1) * group, :] = yacc[
                    f, g * group : (g + 1) * group, :
                ].astype(bf16)
        top[...] = jnp.broadcast_to(jnp.max(peak[...], axis=1, keepdims=True), top.shape)


def exchange_kernel(n_row, n_col, xs, ys, top, xr, yr, tops, sx, rx, sy, ry, st, rt, su, ru, se, re, own):
    me_c = lax.axis_index("col")
    me_r = lax.axis_index("row")
    mesh_id = pl.DeviceIdType.MESH
    barrier = pltpu.get_barrier_semaphore()

    def at_col(d):
        return lax.rem(me_c + d, n_col)

    def at_row(d):
        return lax.rem(me_r + d, n_row)

    for d in range(1, n_col):
        pl.semaphore_signal(barrier, inc=1, device_id=(me_r, at_col(d)), device_id_type=mesh_id)
    for d in range(1, n_row):
        pl.semaphore_signal(barrier, inc=1, device_id=(at_row(d), me_c), device_id_type=mesh_id)
    pl.semaphore_wait(barrier, n_col + n_row - 2)

    def send(src, dst, ssem, rsem, device):
        copy = pltpu.make_async_remote_copy(
            src_ref=src, dst_ref=dst, send_sem=ssem, recv_sem=rsem, device_id=device, device_id_type=mesh_id
        )
        copy.start()
        return copy

    tcopies = [
        send(top, tops.at[me_r, me_c], st.at[d], rt.at[d], (me_r, at_col(d))) for d in range(1, n_col)
    ]
    own_t = pltpu.make_async_copy(top, tops.at[me_r, me_c], own.at[0])
    own_t.start()
    copies = []
    for d in range(1, n_col):
        peer = at_col(d)
        copies.append(send(xs.at[peer], xr.at[me_c], sx.at[d], rx.at[d], (me_r, peer)))
    copies.append(send(xs.at[n_col], xr.at[n_col], se.at[0], re.at[0], (me_r, at_col(1))))
    copies.append(
        send(xs.at[n_col + 1], xr.at[n_col + 1], se.at[1], re.at[1], (me_r, at_col(n_col - 1)))
    )
    for d in range(1, n_row):
        peer = at_row(d)
        copies.append(send(ys.at[peer], yr.at[me_r], sy.at[d], ry.at[d], (peer, me_c)))
    copies.append(send(ys.at[n_row], yr.at[n_row], se.at[2], re.at[2], (at_row(1), me_c)))
    copies.append(
        send(ys.at[n_row + 1], yr.at[n_row + 1], se.at[3], re.at[3], (at_row(n_row - 1), me_c))
    )
    own_x = pltpu.make_async_copy(xs.at[me_c], xr.at[me_c], own.at[1])
    own_y = pltpu.make_async_copy(ys.at[me_r], yr.at[me_r], own.at[2])
    own_x.start()
    own_y.start()
    own_t.wait()
    for copy in tcopies:
        copy.wait()
    ucopies = [
        send(tops.at[me_r], tops.at[me_r], su.at[d], ru.at[d], (at_row(d), me_c)) for d in range(1, n_row)
    ]
    own_x.wait()
    own_y.wait()
    for copy in copies + ucopies:
        copy.wait()


def main_kernel(main, tile, vel, prev, xr, yr, lx, bx, wy, wt, tops, ycol, rhs, inc, thin):
    f = pl.program_id(1)
    rows, width = prev.shape[2], prev.shape[3]
    top = jnp.max(tops[...], axis=(0, 1, 2))
    top = jnp.max(top.reshape(1, top.shape[0]), axis=1, keepdims=True)
    step = cfl_target / (top + 1e-06)
    thin_rows = yr.shape[0] * yr.shape[1]
    thin[0:thin_rows, :] = yr[...].reshape(thin_rows, width)
    if main < rows:
        thin[thin_rows : thin_rows + rows - main, :] = vel[f, 0, main:rows, :]
    lines = xr[...].reshape(xr.shape[0] * xr.shape[1], rows)
    starts = list(range(0, main, tile))
    for start in starts:
        stop = rows if start == starts[-1] else start + tile
        here = slice(start, stop)
        ax = dot(vel[f, 0, here, :], lx[...]) + dot(lines[:, here], bx[0], 0, 0)
        ay0 = dot(wy[0, here, :], vel[f, 0, 0:main, :]) + dot(wt[0, 0, here, :], thin[...])
        ay1 = dot(wy[1, here, :], vel[f, 0, 0:main, :]) + dot(wt[0, 1, here, :], thin[...])
        u = vel[0, 0, here, :].astype(f32)
        v = vel[1, 0, here, :].astype(f32)
        live = ycol[here, 1:2] > 0.0
        total = (ax[:, :width] + ay0) - (u * ax[:, width:] + v * ay1)
        total = jnp.where(live, total, 0.0)
        rhs[0, 0, here, :] = total.astype(bf16)
        change = step * (gamma_coef * total + zeta_coef * prev[0, 0, here, :].astype(f32))
        inc[0, 0, here, :] = jnp.where(live, change, 0.0).astype(bf16)


def per_plane(compact, planes):
    groups = compact.shape[0]
    eye = jnp.eye(planes, dtype=compact.dtype)
    eye = eye.reshape((planes, 1, planes, 1) + (1,) * (compact.ndim - 2))
    wide = compact[None, :, None] * eye
    return wide.reshape((planes, groups * planes * 4) + compact.shape[2:])


def source_weights(coupling, place, own_ends, next_ends, last_hot, prior_ends, first_hot):
    count = coupling.shape[1] // 2
    blocks = coupling.reshape(2, 2 * count, count, 2)

    def col(shift):
        at = lax.rem(place + shift + count, count)
        return lax.dynamic_index_in_dim(blocks, at, 2, keepdims=False)

    own, after, before = col(0), col(1), col(-1)
    total = jnp.zeros((), f32)
    for e in range(2):
        total = total + own[:, :, e, None] * own_ends[:, e, None, :]
        for h in range(2):
            total = total + after[:, :, e, None] * next_ends[h, :, e, None, None] * last_hot[h]
            total = total + before[:, :, e, None] * prior_ends[h, :, e, None, None] * first_hot[h]
    total = total.reshape(2, count, 2, total.shape[-1])
    return jnp.transpose(total, (1, 0, 2, 3)).reshape(count, 4, total.shape[-1])


def shards(
    velocity, rhs_prev, row_counts, x_scale, x_curv, y_scale, y_curv,
    x_local, x_coupling, x_basis, y_local, y_coupling, y_basis,
):
    n_comp, n_plane, rows, width = velocity.shape
    n_col, n_row = lax.axis_size("col"), lax.axis_size("row")
    col_pos, row_pos = lax.axis_index("col"), lax.axis_index("row")
    count = row_counts[row_pos]
    slots = jnp.arange(rows, dtype=jnp.int32)
    live = (slots < count).astype(f32)
    ycol = jnp.stack([y_scale, live], axis=1)

    at_ends = jnp.stack(
        [y_local[:, :, 0], lax.dynamic_index_in_dim(y_local, count - 1, 2, keepdims=False)], axis=2
    ).astype(f32)
    up = [(i, i + 1) for i in range(n_row - 1)]
    down = [(i + 1, i) for i in range(n_row - 1)]
    next_y = lax.ppermute(at_ends[0:2].astype(bf16), "row", down).astype(f32)
    prior_y = lax.ppermute(at_ends[rows + 2 : rows + 4].astype(bf16), "row", up).astype(f32)

    def hot(at, size):
        return (jnp.arange(size, dtype=jnp.int32) == at).astype(f32)

    def edge_groups(first, last):
        zero = jnp.zeros_like(first[0])
        return jnp.stack([jnp.stack(last + [zero, zero]), jnp.stack([zero, zero] + first)])

    first = [hot(h, width) for h in range(2)]
    last = [hot(width - 2 + h, width) for h in range(2)]
    xl = x_local.astype(f32)
    x_ends = jnp.stack([xl[:, :, 0], xl[:, :, width - 1]], axis=2)
    own_ends = jnp.transpose(x_ends[2 : width + 2], (1, 2, 0))
    wx = source_weights(x_coupling, col_pos, own_ends, x_ends[0:2], last, x_ends[width + 2 :], first)
    wx = per_plane(jnp.concatenate([wx, edge_groups(first, last)]), n_plane).astype(bf16)

    def fold_x(a):
        lap = viscosity * (x_scale * x_scale * a[..., 1, :] + x_curv * a[..., 0, :])
        return jnp.concatenate([lap, x_scale * a[..., 0, :]], axis=-1)

    lx_all = fold_x(xl)
    lx = lx_all[2 : width + 2].astype(bf16)
    by_k = jnp.eye(2, dtype=f32)[:, None, :, None]
    bx = fold_x((x_basis[:, :, None, :] * by_k).reshape(4, 2, width))
    zx = jnp.zeros((2, 2 * width), f32)
    bx = jnp.concatenate(
        [
            jnp.broadcast_to(bx, (n_col,) + bx.shape),
            jnp.stack([jnp.concatenate([lx_all[0:2], zx]), jnp.concatenate([zx, lx_all[width + 2 :]])]),
        ]
    )
    bx = per_plane(bx, n_plane).astype(bf16)

    first = [hot(h, rows) for h in range(2)]
    last = [hot(count - 2 + h, rows) for h in range(2)]
    own_ends = jnp.transpose(at_ends[2 : rows + 2], (1, 2, 0)) * live
    wyc = source_weights(y_coupling, row_pos, own_ends, next_y, last, prior_y, first)
    wyc = per_plane(jnp.concatenate([wyc, edge_groups(first, last)]), n_plane).astype(bf16)

    def fold_y(a):
        lap = viscosity * (y_scale * y_scale * a[..., 1, :] + y_curv * a[..., 0, :])
        return jnp.stack([lap, y_scale * a[..., 0, :]], axis=-2)

    yl = y_local.astype(f32)
    tail = rows % 128
    main = rows - tail
    ly = (fold_y(yl[2 : rows + 2]) * live[:, None, None]).astype(bf16)
    wy = jnp.transpose(ly[:main], (1, 2, 0))
    by = fold_y((y_basis[0][:, :, None, :] * by_k).reshape(4, 2, rows))
    zy = jnp.zeros((2, 2, rows), f32)
    low = fold_y(yl[0:2]) * (row_pos > 0).astype(f32)
    high = fold_y(yl[rows + 2 :]) * (row_pos < n_row - 1).astype(f32)
    by = jnp.concatenate(
        [
            jnp.broadcast_to(by, (n_row,) + by.shape),
            jnp.stack([jnp.concatenate([low, zy]), jnp.concatenate([zy, high])]),
        ]
    )
    by = per_plane(by, n_plane).astype(bf16)
    by = jnp.concatenate([by, jnp.broadcast_to(ly[main:], (n_plane,) + ly[main:].shape)], axis=1)
    wt = jnp.transpose(by, (0, 2, 3, 1))

    group = n_plane * 4
    gx, gy = n_col + 2, n_row + 2
    xs_row = x_scale.reshape(1, width)
    limit = 60 * 1024 * 1024
    whole = lambda shape: pl.BlockSpec(shape, lambda *i: (0,) * len(shape))
    by_plane = lambda shape: pl.BlockSpec((1,) + shape[1:], lambda z, *i: (z,) + (0,) * (len(shape) - 1))
    fields = pl.BlockSpec((n_comp, 1, rows, width), lambda z, *i: (0, z, 0, 0))
    xo, yo, top = pl.pallas_call(
        stats_kernel,
        name="stats",
        grid=(n_plane,),
        in_specs=[fields, by_plane(wx.shape), by_plane(wyc.shape), whole(xs_row.shape), whole(ycol.shape)],
        out_specs=[
            whole((gx, n_comp * group, rows)),
            whole((gy, n_comp * group, width)),
            whole((8, 128)),
        ],
        out_shape=[
            jax.ShapeDtypeStruct((gx, n_comp * group, rows), bf16),
            jax.ShapeDtypeStruct((gy, n_comp * group, width), bf16),
            jax.ShapeDtypeStruct((8, 128), f32),
        ],
        scratch_shapes=[
            pltpu.VMEM((n_comp, gx * group, rows), f32),
            pltpu.VMEM((n_comp, gy * group, width), f32),
            pltpu.VMEM((1, width), f32),
        ],
        compiler_params=pltpu.CompilerParams(vmem_limit_bytes=limit),
    )(velocity, wx, wyc, xs_row, ycol)

    dma = pltpu.SemaphoreType.DMA
    anywhere = pl.BlockSpec(memory_space=pl.ANY)
    xr, yr, tops = pl.pallas_call(
        functools.partial(exchange_kernel, n_row, n_col),
        name="exchange",
        in_specs=[anywhere] * 3,
        out_specs=[anywhere] * 3,
        out_shape=[
            jax.ShapeDtypeStruct(xo.shape, bf16),
            jax.ShapeDtypeStruct(yo.shape, bf16),
            jax.ShapeDtypeStruct((n_row, n_col, 8, 128), f32),
        ],
        scratch_shapes=[
            dma((n_col,)), dma((n_col,)), dma((n_row,)), dma((n_row,)), dma((n_col,)), dma((n_col,)),
            dma((n_row,)), dma((n_row,)), dma((4,)), dma((4,)), dma((3,)),
        ],
        compiler_params=pltpu.CompilerParams(collective_id=0, has_side_effects=True),
    )(xo, yo, top)

    one = pl.BlockSpec((1, 1, rows, width), lambda z, f: (f, z, 0, 0))
    tile = 256 if main >= 512 else main
    return pl.pallas_call(
        functools.partial(main_kernel, main, tile),
        name="sub_step",
        grid=(n_plane, n_comp),
        in_specs=[
            fields,
            one,
            pl.BlockSpec((gx, group, rows), lambda z, f: (0, f, 0)),
            pl.BlockSpec((gy, group, width), lambda z, f: (0, f, 0)),
            whole(lx.shape),
            by_plane(bx.shape),
            whole(wy.shape),
            by_plane(wt.shape),
            whole(tops.shape),
            whole(ycol.shape),
        ],
        out_specs=[one, one],
        out_shape=[jax.ShapeDtypeStruct(velocity.shape, bf16)] * 2,
        scratch_shapes=[pltpu.VMEM((gy * group + tail, width), bf16)],
        compiler_params=pltpu.CompilerParams(vmem_limit_bytes=limit),
    )(velocity, rhs_prev, xr, yr, lx, bx, wy, wt, tops, ycol)


def solution(mesh):
    placed = (
        P(None, None, "row", "col"),
        P(None, None, "row", "col"),
        P(),
        P("col"),
        P("col"),
        P("row"),
        P("row"),
        P(),
        P(),
        P(),
        P("row", None, None),
        P(),
        P("row", None, None, None),
    )
    return jax.shard_map(
        shards,
        mesh=mesh,
        in_specs=placed,
        out_specs=(P(None, None, "row", "col"), P(None, None, "row", "col")),
        check_vma=False,
    )
```

time: 612 us -> 155 us (0.25); the launches traced: 600 us -> 155 us
  local copies, waits for them, and re-layouts: 297 us -> 19.9 us
  other arithmetic: 145 us -> 22.2 us
  Pallas kernels: 0 us -> 104 us
  matrix products: 76.6 us -> 0 us
  blocking collectives: 69.6 us -> 0 us
    pallas_call x0 -> x3, Pallas kernels: none -> 104 us  [the longest x1 71.3 us: shards(): pl.pallas_call(functools.partial(main_kernel, main, tile), name='sub_step...]
    slice x12 -> x10, local copies, waits for them, and re-layouts: 87.7 us -> 4.9 us  [the longest x3 2.73 us: shards(): x_ends = jnp.stack([xl[:, :, 0], xl[:, :, width - 1]], axis=2)]
    dot_general x4 -> x0, matrix products: 76.6 us -> none  [the longest x1 40.1 us: shards(): lax.dot_general(y_local.reshape(y_rows + 4, 2 * y_rows), extended, (((0,)...]
    add x2, other arithmetic: 68.8 us -> 0.33 us  [source_weights(): total + before[:, :, e, None] * prior_ends[h, :, e, None, None] * first_h...]
    concatenate x1 -> x0, local copies, waits for them, and re-layouts: 65.5 us -> none  [shards(): extended = jnp.concatenate([rimmed[0:2], stacked, rimmed[6:8]], axis=0)]
    another operation x7 -> x5, local copies, waits for them, and re-layouts: 58.8 us -> 1.75 us  [the longest x2 1.73 us: shards(): ycol = jnp.stack([y_scale, live], axis=1)]
    convert_element_type x2 -> x21, other arithmetic: 62.3 us -> 8.52 us  [the longest x1 1.64 us: shards(): xl = x_local.astype(f32)]
    pmax x1 -> x0, blocking collectives: 41.6 us -> none  [shards(): speed_top = lax.pmax(local_top, ('row', 'col'))]
  transfers between devices with their start and end apart: 4 -> 2, of which waited for: 0 -> 0; matrix products, arithmetic and copies ran while one was open for 56% -> 23% of each run, Pallas kernels for 0% -> 0%
where the time goes in v1:
time: 155 us
  Pallas kernels  104 us (67%)
  other arithmetic  22.2 us (14%)
  local copies, waits for them, and re-layouts  19.9 us (13%)
  starting transfers between devices  5.93 us (4%)
  between operations  3.3 us (2%)
    pallas_call x1, Pallas kernels, shards(): pl.pallas_call(functools.partial(main_kernel, main, tile), name='sub_step...  71.3 us
    pallas_call x1, Pallas kernels, shards(): pl.pallas_call(functools.partial(exchange_kernel, n_row, n_col), name='ex...  17.8 us
    pallas_call x1, Pallas kernels, shards(): pl.pallas_call(stats_kernel, name='stats', grid=(n_plane,), in_specs=[fie...  14.5 us
    mul x4, other arithmetic, fold_y(): lap = viscosity * (y_scale * y_scale * a[..., 1, :] + y_curv * a[..., 0, :])  6.87 us
    ppermute x1, starting transfers between devices, shards(): lax.ppermute(at_ends[rows + 2:rows + 4].astype(bf16), 'row', up).astype(f32)  4.65 us
  transfers between devices with their start and end apart: 2, of which 0 were waited for; matrix products, arithmetic and copies ran while one was open for 23% of the time, Pallas kernels for 0%

profile of v1, /device:TPU:1, one launch (start us, length us, event | category | flops | bytes accessed | tf_op | source)
XLA Modules:
  0.0 154.8 jit_solution(1794917147021730147)
XLA Ops:
  0.6 1.2 dynamic_slice.31
  3.2 0.8 fusion.33
  4.1 1.3 collective-permute-start
  5.4 4.6 %collective-permute-start.1 = (bf16[2,2,2]{0,2,1:T(2,128)(2,1)S(1)}, bf16[2,2,2]{0,2,1:T(2,128)(2,1)S(1)}, u32[]{:S(2)}, u32[]{:S(2)}) collective-permute-start(bf16[2,2,2]{0,2,1:T(2,128)(2,1)S(1)} %get-tuple-element.71), channel_id=1, source_target_pairs={{0,8},{8,16},{16,24},{1,9},{9,17},{17,25},{2,10},{10,18},{18,26},{... | collective-permute-start | bytes 56 | tf_op jit(solution)/shard_map/ppermute | solution.py:199
  12.2 0.8 mul.1190
  13.6 1.6 %copy_convert_fusion = f32[516,2,512]{2,0,1:T(8,128)S(1)} fusion(bf16[516,2,512]{2,1,0:T(2,128)(2,1)} %param.20), kind=kLoop, calls=%fused_computation.23 | loop fusion | flops 528384 | bytes 3170304 | tf_op jit(solution)/shard_map/convert_element_type | solution.py:210
  15.5 1.2 fusion.34
  17.4 2.2 %fusion.12 = (f32[2,1,1032]{0,2,1:T(8,128)}, f32[2,1,1032]{0,2,1:T(8,128)}, f32[2,1,1032]{0,2,1:T(8,128)}, f32[2,1,1032]{0,2,1:T(8,128)}) fusion(f32[1036,2,1032]{0,2,1:T(8,128)S(1)} %convert_element_type.252, f32[1032]{0:T(1024)S(1)} %mul.1190, f32[1032]{0:T(1024)S(1)} %copy-done.9, f32[1032]{0:T(1024)S(1)} %copy-done.8), kind=kLoop, calls=%fused_computation.30 | loop fusion | flops 20640 | bytes 78432 | tf_op jit(solution)/shard_map/mul | solution.py:240
  19.5 3.9 %fusion.2 = (f32[1032,1,1032]{0,2,1:T(8,128)S(1)}, f32[1032,1,1032]{0,2,1:T(8,128)S(1)}) fusion(f32[1036,2,1032]{0,2,1:T(8,128)S(1)} %convert_element_type.252, f32[1032]{0:T(1024)S(1)} %copy-done.9, f32[1032]{0:T(1024)S(1)} %mul.1190, f32[1032]{0:T(1024)S(1)} %copy-done.8), kind=kLoop, calls=%fused_computation.4 | loop fusion | flops 5325120 | bytes 17052768 | tf_op jit(solution)/shard_map/mul | solution.py:240
  23.5 1.2 fusion
  24.7 0.8 slice.336
  25.6 2.5 %slice_bitcast_fusion.wy = bf16[2,1032,1024]{2,1,0:T(8,128)(2,1)} fusion(bf16[1032,2,1032]{0,2,1:T(8,128)(2,1)S(1)} %fusion), kind=kLoop, calls=%fused_computation.6 | loop fusion | bytes 8454144 | tf_op jit(solution)/shard_map/transpose | solution.py:247
  28.5 1.3 fusion.8
  30.7 1.0 copy.209.ycol
  34.4 1.3 copy.168
  36.2 1.3 fusion.4.lx
  38.5 1.0 multiply_convert_fusion.3.wx
  39.5 1.3 multiply_convert_fusion.1.bx
  42.2 0.9 copy.219
  43.8 2.5 %maximum_bitcast_fusion.wt = bf16[4,2,1032,104]{3,2,1,0:T(8,128)(2,1)} fusion(bf16[4,8,2,1032]{1,3,2,0:T(8,128)(2,1)S(1)} %broadcast_in_dim.8, bf16[4,96,2,1032]{1,3,2,0:T(8,128)(2,1)S(1)} %multiply_convert_fusion), kind=kLoop, calls=%fused_computation.13 | loop fusion | flops 3434496 | bytes 3434496 | tf_op jit(solution)/shard_map/transpose | solution.py:260
  50.2 1.1 multiply_convert_fusion.2.wy
  51.3 14.5 %stats.1 = (bf16[10,48,1032]{2,1,0:T(8,128)(2,1)}, bf16[6,48,512]{2,1,0:T(8,128)(2,1)}, f32[8,128]{1,0:T(8,128)}) custom-call(bf16[3,4,1032,512]{3,2,1,0:T(8,128)(2,1)} %vel.3, bf16[4,160,512]{2,1,0:T(8,128)(2,1)} %multiply_convert_fusion.3.wx, bf16[4,96,1032]{2,1,0:T(8,128)(2,1)} %multiply_convert_fusion.2.wy, f32[1,512]{1,0:T(1,128)} %bitcast.120, ...), custom_call_target="tpu_custom_call" | custom-call | tf_op jit(solution)/shard_map/stats/pallas_call | solution.py:269
  65.7 17.8 %exchange.1 = (bf16[10,48,1032]{2,1,0:T(8,128)(2,1)}, bf16[6,48,512]{2,1,0:T(8,128)(2,1)}, f32[4,8,8,128]{3,2,1,0:T(8,128)}) custom-call(bf16[10,48,1032]{2,1,0:T(8,128)(2,1)} %get-tuple-element.8.xs, bf16[6,48,512]{2,1,0:T(8,128)(2,1)} %get-tuple-element.9.ys, f32[8,128]{1,0:T(8,128)} %get-tuple-element.10.top), custom_call_target="tpu_custom_call" | custom-call | tf_op jit(solution)/shard_map/exchange/pallas_call | solution.py:294
  83.5 71.3 %sub_step.1 = (bf16[3,4,1032,512]{3,2,1,0:T(8,128)(2,1)}, bf16[3,4,1032,512]{3,2,1,0:T(8,128)(2,1)}) custom-call(bf16[3,4,1032,512]{3,2,1,0:T(8,128)(2,1)} %vel.3, bf16[3,4,1032,512]{3,2,1,0:T(8,128)(2,1)} %prev.1, bf16[10,48,1032]{2,1,0:T(8,128)(2,1)} %get-tuple-element.11.xr, bf16[6,48,512]{2,1,0:T(8,128)(2,1)} %get-tuple-element.12.yr, ...), custom_call_target="tpu_custom_call" | custom-call | tf_op jit(solution)/shard_map/sub_step/pallas_call | solution.py:313
  (185 shorter events, 14.0 us)
Async XLA Ops:
  4.1 42.3 %collective-permute-start = (bf16[2,2,2]{0,2,1:T(2,128)(2,1)S(1)}, bf16[2,2,2]{0,2,1:T(2,128)(2,1)S(1)}, u32[]{:S(2)}, u32[]{:S(2)}) collective-permute-start(bf16[2,2,2]{0,2,1:T(2,128)(2,1)S(1)} %get-tuple-element.70), channel_id=1, source_target_pairs={{8,0},{16,8},{24,16},{9,1},{17,9},{25,17},{10,2},{18,10},{26,18},{... | collective-permute-start | bytes 56 | tf_op jit(solution)/shard_map/ppermute | solution.py:198
  5.4 42.4 %collective-permute-start.1 = (bf16[2,2,2]{0,2,1:T(2,128)(2,1)S(1)}, bf16[2,2,2]{0,2,1:T(2,128)(2,1)S(1)}, u32[]{:S(2)}, u32[]{:S(2)}) collective-permute-start(bf16[2,2,2]{0,2,1:T(2,128)(2,1)S(1)} %get-tuple-element.71), channel_id=1, source_target_pairs={{0,8},{8,16},{16,24},{1,9},{9,17},{17,25},{2,10},{10,18},{18,26},{... | collective-permute-start | bytes 56 | tf_op jit(solution)/shard_map/ppermute | solution.py:199
  13.6 3.0 %copy-start.1 = (bf16[1036,2,1032]{0,2,1:T(8,128)(2,1)S(1)}, bf16[1036,2,1032]{0,2,1:T(8,128)(2,1)}, u32[]{:S(2)}) copy-start(bf16[1036,2,1032]{0,2,1:T(8,128)(2,1)} %param.23) | copy-start | bytes 12829828
  16.6 0.7 copy-start.8
  16.6 0.7 copy-start.9
  25.6 2.7 %copy-start.10 = (f32[512]{0:T(512)S(1)}, f32[512]{0:T(512)}, u32[]{:S(2)}) copy-start(f32[512]{0:T(512)} %param.16) | copy-start | bytes 6148
  25.6 2.8 %copy-start.14 = (f32[2,2,512]{2,1,0:T(2,128)S(1)}, f32[2,2,512]{2,1,0:T(2,128)}, u32[]{:S(2)}) copy-start(f32[2,2,512]{2,1,0:T(2,128)} %param.22) | copy-start | bytes 24580
  25.6 2.9 %copy-start.13 = (f32[512]{0:T(512)S(1)}, f32[512]{0:T(512)}, u32[]{:S(2)}) copy-start(f32[512]{0:T(512)} %param.17) | copy-start | bytes 6148
  28.5 1.4 copy-start.15
  28.5 1.5 copy-start.12
  28.5 1.7 %copy-start.11 = (f32[1,2,2,1032]{3,2,1,0:T(2,128)S(1)}, f32[1,2,2,1032]{3,2,1,0:T(2,128)}, u32[]{:S(2)}) copy-start(f32[1,2,2,1032]{3,2,1,0:T(2,128)} %param.25) | copy-start | bytes 49540
  29.8 6.0 %copy-start.2 = (f32[516,2,1]{2,0,1:T(8,128)S(1)}, f32[516,2,1]{2,0,1:T(8,128)}, u32[]{:S(2)}) copy-start(f32[516,2,1]{2,0,1:T(8,128)} %get-tuple-element.65) | copy-start | bytes 12388
  29.8 6.4 %copy-start = (f32[516,512]{1,0:T(8,128)S(1)}, f32[516,512]{1,0:T(8,128)}, u32[]{:S(2)}) copy-start(f32[516,512]{1,0:T(8,128)} %get-tuple-element.63) | copy-start | bytes 3170308
  34.4 3.1 %copy-start.16 = (pred[4]{0:T(512)(128)(4,1)S(1)}, pred[4]{0:T(512)(128)(4,1)}, u32[]{:S(2)}) copy-start(pred[4]{0:T(512)(128)(4,1)} %constant.86.clone.1) | copy-start | bytes 16
  38.2 2.5 %copy-start.7 = (f32[2,1,1032]{0,2,1:T(8,128)S(1)}, f32[2,1,1032]{0,2,1:T(8,128)}, u32[]{:S(2)}) copy-start(f32[2,1,1032]{0,2,1:T(8,128)} %get-tuple-element.50) | copy-start | bytes 24772
  38.2 2.7 %copy-start.6 = (f32[2,1,1032]{0,2,1:T(8,128)S(1)}, f32[2,1,1032]{0,2,1:T(8,128)}, u32[]{:S(2)}) copy-start(f32[2,1,1032]{0,2,1:T(8,128)} %get-tuple-element.51) | copy-start | bytes 24772
  38.5 2.7 %copy-start.5 = (f32[2,1,1032]{0,2,1:T(8,128)S(1)}, f32[2,1,1032]{0,2,1:T(8,128)}, u32[]{:S(2)}) copy-start(f32[2,1,1032]{0,2,1:T(8,128)} %get-tuple-element.54) | copy-start | bytes 24772
  38.5 2.9 %copy-start.4 = (f32[2,1,1032]{0,2,1:T(8,128)S(1)}, f32[2,1,1032]{0,2,1:T(8,128)}, u32[]{:S(2)}) copy-start(f32[2,1,1032]{0,2,1:T(8,128)} %get-tuple-element.55) | copy-start | bytes 24772
  42.2 1.3 copy-start.3

commit v2 on v1

v2 whole, which is shorter than its diff:
```python
import functools
import jax
import jax.numpy as jnp
import numpy as np
from jax import lax
from jax.experimental import pallas as pl
from jax.experimental.pallas import tpu as pltpu
from jax.sharding import PartitionSpec as P

viscosity = 0.1
cfl_target = 1.5
gamma_coef = 5.0 / 12.0
zeta_coef = -17.0 / 60.0
f32 = jnp.float32
bf16 = jnp.bfloat16


def dot(a, b, ca=1, cb=0):
    return lax.dot_general(a, b, (((ca,), (cb,)), ((), ())), preferred_element_type=f32)


def split(a):
    high = a.astype(bf16)
    return high, (a - high.astype(f32)).astype(bf16)


def combine(mix, parts):
    mh, ml = split(mix)
    ph, pw = split(parts)
    return dot(mh, ph) + dot(ml, ph) + dot(mh, pw)


def stats_kernel(vel, dx, dy, mx, my, xs, ycol, xo, yo, top, xg, yg, peak):
    z = pl.program_id(0)
    speed = (
        jnp.abs(vel[0, 0].astype(f32)) * xs[...] + jnp.abs(vel[1, 0].astype(f32)) * ycol[:, 0:1]
    ) * ycol[:, 1:2]
    best = jnp.max(speed, axis=0, keepdims=True)
    for f in range(vel.shape[0]):
        block = vel[f, 0]
        xg[f, z] = dot(dx[...], block, 1, 1)
        yg[f, z] = dot(dy[...], block)

    @pl.when(z == 0)
    def _():
        peak[...] = best

    @pl.when(z > 0)
    def _():
        peak[...] = jnp.maximum(peak[...], best)

    @pl.when(z == pl.num_programs(0) - 1)
    def _():
        group = xo.shape[1] // vel.shape[0]
        for f in range(vel.shape[0]):
            for out, mix, parts in ((xo, mx, xg), (yo, my, yg)):
                flat = parts[f].reshape(parts.shape[1] * 8, parts.shape[3])
                total = combine(mix[...], flat).astype(bf16)
                out[:, f * group : (f + 1) * group, :] = total.reshape(
                    out.shape[0], group, out.shape[2]
                )
        top[...] = jnp.broadcast_to(jnp.max(peak[...], axis=1, keepdims=True), top.shape)


def prepare(xt, yt, xrow, ycol, livek, bx8, by8, sx, s1, s2, s3, lx, bx, wy, wt):
    width = xt.shape[2]
    rows, main = wy.shape[1], wy.shape[2]
    planes, thin = wt.shape[0], wt.shape[3]
    a0 = xt[0].astype(f32)
    a1 = xt[1].astype(f32)
    xs, xc = xrow[0:1, :], xrow[1:2, :]
    lx[:, :width] = (viscosity * (xs * xs * a1 + xc * a0))[2 : width + 2].astype(bf16)
    lx[:, width:] = (xs * a0)[2 : width + 2].astype(bf16)
    bx[...] = dot(sx[...], bx8[...].astype(bf16)).astype(bf16).reshape(bx.shape)
    starts = list(range(0, main, 128))
    for start in starts:
        stop = rows if start == starts[-1] else start + 128
        here = slice(start, stop)
        b0 = yt[0, here, :].astype(f32) * livek[...]
        b1 = yt[1, here, :].astype(f32) * livek[...]
        ys, yc = ycol[here, 0:1], ycol[here, 2:3]
        for q, fold in enumerate((viscosity * (ys * ys * b1 + yc * b0), ys * b0)):
            wy[q, here, :] = fold[:, 2 : main + 2].astype(bf16)
            small = fold.astype(bf16)
            wide = (
                dot(by8[q, :, here].astype(bf16), s1[...], 0, 0)
                + dot(small[:, 0:128], s2[...])
                + dot(small[:, main:], s3[...])
            ).astype(bf16)
            for z in range(planes):
                wt[z, q, here, :] = wide[:, z * thin : (z + 1) * thin]


def exchange_kernel(n_row, n_col, *refs):
    xs, ys, top = refs[:3]
    sources = refs[3:14]
    xr, yr, tops = refs[14:17]
    weights = refs[17:21]
    sx, rx, sy, ry, st, rt, su, ru, se, re, own = refs[21:]
    me_c = lax.axis_index("col")
    me_r = lax.axis_index("row")
    mesh_id = pl.DeviceIdType.MESH
    barrier = pltpu.get_barrier_semaphore()

    def at_col(d):
        return lax.rem(me_c + d, n_col)

    def at_row(d):
        return lax.rem(me_r + d, n_row)

    for d in range(1, n_col):
        pl.semaphore_signal(barrier, inc=1, device_id=(me_r, at_col(d)), device_id_type=mesh_id)
    for d in range(1, n_row):
        pl.semaphore_signal(barrier, inc=1, device_id=(at_row(d), me_c), device_id_type=mesh_id)
    pl.semaphore_wait(barrier, n_col + n_row - 2)

    def send(src, dst, ssem, rsem, device):
        copy = pltpu.make_async_remote_copy(
            src_ref=src, dst_ref=dst, send_sem=ssem, recv_sem=rsem, device_id=device, device_id_type=mesh_id
        )
        copy.start()
        return copy

    tcopies = [
        send(top, tops.at[me_r, me_c], st.at[d], rt.at[d], (me_r, at_col(d))) for d in range(1, n_col)
    ]
    own_t = pltpu.make_async_copy(top, tops.at[me_r, me_c], own.at[0])
    own_t.start()
    copies = []
    for d in range(1, n_col):
        peer = at_col(d)
        copies.append(send(xs.at[peer], xr.at[me_c], sx.at[d], rx.at[d], (me_r, peer)))
    copies.append(send(xs.at[n_col], xr.at[n_col], se.at[0], re.at[0], (me_r, at_col(1))))
    copies.append(
        send(xs.at[n_col + 1], xr.at[n_col + 1], se.at[1], re.at[1], (me_r, at_col(n_col - 1)))
    )
    for d in range(1, n_row):
        peer = at_row(d)
        copies.append(send(ys.at[peer], yr.at[me_r], sy.at[d], ry.at[d], (peer, me_c)))
    copies.append(send(ys.at[n_row], yr.at[n_row], se.at[2], re.at[2], (at_row(1), me_c)))
    copies.append(
        send(ys.at[n_row + 1], yr.at[n_row + 1], se.at[3], re.at[3], (at_row(n_row - 1), me_c))
    )
    own_x = pltpu.make_async_copy(xs.at[me_c], xr.at[me_c], own.at[1])
    own_y = pltpu.make_async_copy(ys.at[me_r], yr.at[me_r], own.at[2])
    own_x.start()
    own_y.start()
    own_t.wait()
    for copy in tcopies:
        copy.wait()
    ucopies = [
        send(tops.at[me_r], tops.at[me_r], su.at[d], ru.at[d], (at_row(d), me_c)) for d in range(1, n_row)
    ]
    prepare(*sources, *weights)
    own_x.wait()
    own_y.wait()
    for copy in copies + ucopies:
        copy.wait()


def main_kernel(main, tile, vel, prev, xr, yr, lx, bx, wy, wt, tops, ycol, rhs, inc, thin):
    f = pl.program_id(1)
    rows, width = prev.shape[2], prev.shape[3]
    top = jnp.max(tops[...], axis=(0, 1, 2))
    top = jnp.max(top.reshape(1, top.shape[0]), axis=1, keepdims=True)
    step = cfl_target / (top + 1e-06)
    thin_rows = yr.shape[0] * yr.shape[1]
    thin[0:thin_rows, :] = yr[...].reshape(thin_rows, width)
    if main < rows:
        thin[thin_rows : thin_rows + rows - main, :] = vel[f, 0, main:rows, :]
    filled = thin_rows + rows - main
    if filled < thin.shape[0]:
        thin[filled:, :] = jnp.zeros((thin.shape[0] - filled, width), bf16)
    lines = xr[...].reshape(xr.shape[0] * xr.shape[1], rows)
    starts = list(range(0, main, tile))
    for start in starts:
        stop = rows if start == starts[-1] else start + tile
        here = slice(start, stop)
        ax = dot(vel[f, 0, here, :], lx[...]) + dot(lines[:, here], bx[0], 0, 0)
        ay0 = dot(wy[0, here, :], vel[f, 0, 0:main, :]) + dot(wt[0, 0, here, :], thin[...])
        ay1 = dot(wy[1, here, :], vel[f, 0, 0:main, :]) + dot(wt[0, 1, here, :], thin[...])
        u = vel[0, 0, here, :].astype(f32)
        v = vel[1, 0, here, :].astype(f32)
        live = ycol[here, 1:2] > 0.0
        total = (ax[:, :width] + ay0) - (u * ax[:, width:] + v * ay1)
        total = jnp.where(live, total, 0.0)
        rhs[0, 0, here, :] = total.astype(bf16)
        change = step * (gamma_coef * total + zeta_coef * prev[0, 0, here, :].astype(f32))
        inc[0, 0, here, :] = jnp.where(live, change, 0.0).astype(bf16)


def source_mix(coupling, place, next_ends, prior_ends, planes):
    count = coupling.shape[1] // 2
    blocks = coupling.reshape(2, 2 * count, count, 2)

    def col(shift):
        at = lax.rem(place + shift + count, count)
        return lax.dynamic_index_in_dim(blocks, at, 2, keepdims=False)

    own = col(0)[:, :, None, :] * jnp.eye(2, dtype=f32)[:, None, :, None]
    own = own.reshape(2, 2 * count, 4)
    first = jnp.sum(col(-1)[:, :, None, :] * jnp.transpose(prior_ends, (1, 0, 2))[:, None], axis=3)
    last = jnp.sum(col(1)[:, :, None, :] * jnp.transpose(next_ends, (1, 0, 2))[:, None], axis=3)
    mix = jnp.concatenate([own, first, last], axis=2).reshape(2, count, 2, 8)
    mix = jnp.transpose(mix, (1, 0, 2, 3)).reshape(count, 4, 8)
    edges = np.zeros((2, 4, 8), np.float32)
    edges[0, 0, 6] = edges[0, 1, 7] = edges[1, 2, 4] = edges[1, 3, 5] = 1.0
    mix = jnp.concatenate([mix, edges])
    wide = mix[:, None, :, None, :] * np.eye(planes, dtype=np.float32)[None, :, None, :, None]
    return wide.reshape((count + 2) * planes * 4, planes * 8)


def shards(
    velocity, rhs_prev, row_counts, x_scale, x_curv, y_scale, y_curv,
    x_local, x_coupling, x_basis, y_local, y_coupling, y_basis,
):
    n_comp, n_plane, rows, width = velocity.shape
    n_col, n_row = lax.axis_size("col"), lax.axis_size("row")
    col_pos, row_pos = lax.axis_index("col"), lax.axis_index("row")
    group = n_plane * 4
    gx, gy = n_col + 2, n_row + 2
    tail = rows % 128
    main = rows - tail
    count = row_counts[row_pos]
    slots = jnp.arange(rows, dtype=jnp.int32)
    live = (slots < count).astype(f32)
    ycol = jnp.stack([y_scale, live, y_curv], axis=1)
    yt = jnp.transpose(y_local, (1, 2, 0))
    xt = jnp.transpose(x_local, (1, 0, 2))

    y_ends = jnp.stack(
        [yt[:, 0, :], lax.dynamic_index_in_dim(yt, count - 1, 1, keepdims=False)], axis=1
    )
    up = [(i, i + 1) for i in range(n_row - 1)]
    down = [(i + 1, i) for i in range(n_row - 1)]
    next_y = lax.ppermute(y_ends[:, :, 0:2], "row", down).astype(f32)
    prior_y = lax.ppermute(y_ends[:, :, rows + 2 :], "row", up).astype(f32)
    x_ends = jnp.stack([x_local[:, :, 0], x_local[:, :, width - 1]], axis=2)
    x_ends_f = x_ends.astype(f32)

    def hot(at, size):
        return (jnp.arange(size, dtype=jnp.int32) == at).astype(bf16)

    dx = jnp.concatenate(
        [
            jnp.transpose(x_ends[2 : width + 2], (1, 2, 0)).reshape(4, width),
            jnp.stack([hot(0, width), hot(1, width), hot(width - 2, width), hot(width - 1, width)]),
        ]
    )
    dy = jnp.concatenate(
        [
            (y_ends[:, :, 2 : rows + 2] * live.astype(bf16)).reshape(4, rows),
            jnp.stack([hot(0, rows), hot(1, rows), hot(count - 2, rows), hot(count - 1, rows)]),
        ]
    )
    mx = source_mix(x_coupling, col_pos, x_ends_f[0:2], x_ends_f[width + 2 :], n_plane)
    my = source_mix(
        y_coupling, row_pos, jnp.transpose(next_y, (2, 0, 1)), jnp.transpose(prior_y, (2, 0, 1)), n_plane
    )

    def fold_x(a0, a1):
        lap = viscosity * (x_scale * x_scale * a1 + x_curv * a0)
        return jnp.concatenate([lap, x_scale * a0], axis=-1)

    def fold_y(a0, a1):
        return jnp.stack([viscosity * (y_scale * y_scale * a1 + y_curv * a0), y_scale * a0])

    def by_k(basis):
        zero = jnp.zeros_like(basis[0])
        return jnp.concatenate([basis[0], zero]), jnp.concatenate([zero, basis[1]])

    edge = jnp.concatenate([xt[:, 0:2], xt[:, width + 2 :]], axis=1).astype(f32)
    x0, x1 = by_k(x_basis)
    bx8 = fold_x(jnp.concatenate([x0, edge[0]]), jnp.concatenate([x1, edge[1]]))
    y0, y1 = by_k(y_basis[0])
    by8 = jnp.pad(fold_y(y0, y1), ((0, 0), (0, 4), (0, 0)))
    place = jnp.arange(rows + 4, dtype=jnp.int32) - 2
    livek = jnp.logical_and(place < count, jnp.logical_or(place >= 0, row_pos > 0))
    livek = jnp.logical_or(livek, jnp.logical_and(place >= rows, row_pos < n_row - 1))
    livek = livek.astype(f32)[None, :]
    xrow = jnp.stack([x_scale, x_curv])

    thin = -(-(gy * group + tail) // 128) * 128
    sx = np.zeros((n_plane, gx, n_plane, 4, 8), np.float32)
    s1 = np.zeros((8, n_plane, thin), np.float32)
    s2 = np.zeros((128, n_plane, thin), np.float32)
    s3 = np.zeros((tail + 4, n_plane, thin), np.float32)
    for z in range(n_plane):
        for c in range(4):
            sx[z, :n_col, z, c, c] = 1.0
            s1[c, z, np.arange(n_row) * group + z * 4 + c] = 1.0
        for h in range(2):
            sx[z, n_col, z, h, 4 + h] = 1.0
            sx[z, n_col + 1, z, 2 + h, 6 + h] = 1.0
            s2[h, z, n_row * group + z * 4 + h] = 1.0
            s3[tail + 2 + h, z, (n_row + 1) * group + z * 4 + 2 + h] = 1.0
        for t in range(tail):
            s3[2 + t, z, gy * group + t] = 1.0
    sx = jnp.asarray(sx.reshape(-1, 8), bf16)
    s1, s2, s3 = (jnp.asarray(s.reshape(s.shape[0], -1), bf16) for s in (s1, s2, s3))

    xs_row = x_scale.reshape(1, width)
    limit = 60 * 1024 * 1024
    whole = lambda shape: pl.BlockSpec(shape, lambda *i: (0,) * len(shape))
    by_plane = lambda shape: pl.BlockSpec((1,) + shape[1:], lambda z, *i: (z,) + (0,) * (len(shape) - 1))
    fields = pl.BlockSpec((n_comp, 1, rows, width), lambda z, *i: (0, z, 0, 0))
    xo, yo, top = pl.pallas_call(
        stats_kernel,
        name="stats",
        grid=(n_plane,),
        in_specs=[fields] + [whole(a.shape) for a in (dx, dy, mx, my, xs_row, ycol)],
        out_specs=[
            whole((gx, n_comp * group, rows)),
            whole((gy, n_comp * group, width)),
            whole((8, 128)),
        ],
        out_shape=[
            jax.ShapeDtypeStruct((gx, n_comp * group, rows), bf16),
            jax.ShapeDtypeStruct((gy, n_comp * group, width), bf16),
            jax.ShapeDtypeStruct((8, 128), f32),
        ],
        scratch_shapes=[
            pltpu.VMEM((n_comp, n_plane, 8, rows), f32),
            pltpu.VMEM((n_comp, n_plane, 8, width), f32),
            pltpu.VMEM((1, width), f32),
        ],
        compiler_params=pltpu.CompilerParams(vmem_limit_bytes=limit),
    )(velocity, dx, dy, mx, my, xs_row, ycol)

    dma = pltpu.SemaphoreType.DMA
    anywhere = pl.BlockSpec(memory_space=pl.ANY)
    in_vmem = pl.BlockSpec(memory_space=pltpu.VMEM)
    sources = (xt, yt, xrow, ycol, livek, bx8, by8, sx, s1, s2, s3)
    xr, yr, tops, lx, bx, wy, wt = pl.pallas_call(
        functools.partial(exchange_kernel, n_row, n_col),
        name="exchange",
        in_specs=[anywhere] * 3 + [in_vmem] * len(sources),
        out_specs=[anywhere] * 3 + [in_vmem] * 4,
        out_shape=[
            jax.ShapeDtypeStruct(xo.shape, bf16),
            jax.ShapeDtypeStruct(yo.shape, bf16),
            jax.ShapeDtypeStruct((n_row, n_col, 8, 128), f32),
            jax.ShapeDtypeStruct((width, 2 * width), bf16),
            jax.ShapeDtypeStruct((n_plane, gx * group, 2 * width), bf16),
            jax.ShapeDtypeStruct((2, rows, main), bf16),
            jax.ShapeDtypeStruct((n_plane, 2, rows, thin), bf16),
        ],
        scratch_shapes=[
            dma((n_col,)), dma((n_col,)), dma((n_row,)), dma((n_row,)), dma((n_col,)), dma((n_col,)),
            dma((n_row,)), dma((n_row,)), dma((4,)), dma((4,)), dma((3,)),
        ],
        compiler_params=pltpu.CompilerParams(
            collective_id=0, has_side_effects=True, vmem_limit_bytes=limit
        ),
    )(xo, yo, top, *sources)

    one = pl.BlockSpec((1, 1, rows, width), lambda z, f: (f, z, 0, 0))
    tile = 256 if main >= 512 else main
    return pl.pallas_call(
        functools.partial(main_kernel, main, tile),
        name="sub_step",
        grid=(n_plane, n_comp),
        in_specs=[
            fields,
            one,
            pl.BlockSpec((gx, group, rows), lambda z, f: (0, f, 0)),
            pl.BlockSpec((gy, group, width), lambda z, f: (0, f, 0)),
            whole(lx.shape),
            by_plane(bx.shape),
            whole(wy.shape),
            by_plane(wt.shape),
            whole(tops.shape),
            whole(ycol.shape),
        ],
        out_specs=[one, one],
        out_shape=[jax.ShapeDtypeStruct(velocity.shape, bf16)] * 2,
        scratch_shapes=[pltpu.VMEM((thin, width), bf16)],
        compiler_params=pltpu.CompilerParams(vmem_limit_bytes=limit),
    )(velocity, rhs_prev, xr, yr, lx, bx, wy, wt, tops, ycol)


def solution(mesh):
    placed = (
        P(None, None, "row", "col"),
        P(None, None, "row", "col"),
        P(),
        P("col"),
        P("col"),
        P("row"),
        P("row"),
        P(),
        P(),
        P(),
        P("row", None, None),
        P(),
        P("row", None, None, None),
    )
    return jax.shard_map(
        shards,
        mesh=mesh,
        in_specs=placed,
        out_specs=(P(None, None, "row", "col"), P(None, None, "row", "col")),
        check_vma=False,
    )
```

time: 155 us -> 136 us (0.88)
  other arithmetic: 22.2 us -> 6.36 us
  local copies, waits for them, and re-layouts: 19.9 us -> 12 us
  Pallas kernels: 104 us -> 108 us
    pallas_call x1, Pallas kernels: 17.8 us -> 25.7 us  [shards(): pl.pallas_call(functools.partial(exchange_kernel, n_row, n_col), name='ex...]
    mul x14 -> x8, other arithmetic: 8.72 us -> 1.28 us  [the longest x1 0.77 us: fold_y(): y_scale * y_scale * a1 + y_curv * a0]
    mul x89 -> x12, local copies, waits for them, and re-layouts: 8.8 us -> 2.25 us  [the longest x2 1.56 us: source_mix(): mix[:, None, :, None, :]]
    convert_element_type x19 -> x9, other arithmetic: 7.21 us -> 1.98 us  [the longest x1 1.26 us: shards(): livek = livek.astype(f32)[None, :]]
    pallas_call x1, Pallas kernels: 14.5 us -> 11.4 us  [shards(): pl.pallas_call(stats_kernel, name='stats', grid=(n_plane,), in_specs=[fie...]
    slice x10 -> x3, local copies, waits for them, and re-layouts: 4.9 us -> 2.3 us  [the longest x1 1.51 us: shards(): x_ends = jnp.stack([x_local[:, :, 0], x_local[:, :, width - 1]], axis=2)]
    transpose x2, other arithmetic: 2.64 us -> 0.18 us  [the longest x1 0.1 us: shards(): jnp.transpose(x_ends[2:width + 2], (1, 2, 0)).reshape(4, width)]
    concatenate x0 -> x11, local copies, waits for them, and re-layouts: none -> 2.28 us  [the longest x8 1 us: source_mix(): mix = jnp.concatenate([own, first, last], axis=2).reshape(2, count, 2, 8)]
  transfers between devices with their start and end apart: 2 -> 2, of which waited for: 0 -> 0; matrix products, arithmetic and copies ran while one was open for 23% -> 10% of each run, Pallas kernels for 0% -> 0%
where the time goes in v2:
time: 136 us; the launch traced here: 135 us
  Pallas kernels  108 us (79%)
  local copies, waits for them, and re-layouts  12 us (9%)
  other arithmetic  6.36 us (5%)
  starting transfers between devices  5.3 us (4%)
  between operations  3.04 us (2%)
    pallas_call x1, Pallas kernels, shards(): pl.pallas_call(functools.partial(main_kernel, main, tile), name='sub_step...  71.2 us
    pallas_call x1, Pallas kernels, shards(): pl.pallas_call(functools.partial(exchange_kernel, n_row, n_col), name='ex...  25.7 us
    pallas_call x1, Pallas kernels, shards(): pl.pallas_call(stats_kernel, name='stats', grid=(n_plane,), in_specs=[fie...  11.4 us
    ppermute x1, starting transfers between devices, shards(): prior_y = lax.ppermute(y_ends[:, :, rows + 2:], 'row', up).astype(f32)  4.01 us
  transfers between devices with their start and end apart: 2, of which 0 were waited for; matrix products, arithmetic and copies ran while one was open for 10% of the time, Pallas kernels for 0%

profile of v2, /device:TPU:1, one launch (start us, length us, event | category | flops | bytes accessed | tf_op | source)
XLA Modules:
  0.0 135.1 jit_solution(16050955365959357547)
XLA Ops:
  0.7 1.3 dynamic_slice.27
  3.3 0.8 dynamic-slice_bitcast_fusion
  4.1 0.8 slice.72
  5.0 4.0 %collective-permute-start = (bf16[2,2,2]{2,1,0:T(2,128)(2,1)S(1)}, bf16[2,2,2]{2,1,0:T(2,128)(2,1)S(1)}, u32[]{:S(2)}, u32[]{:S(2)}) collective-permute-start(bf16[2,2,2]{2,1,0:T(2,128)(2,1)S(1)} %get-tuple-element.28), channel_id=1, source_target_pairs={{0,8},{8,16},{16,24},{1,9},{9,17},{17,25},{2,10},{10,18},{18,26},{... | collective-permute-start | bytes 56 | tf_op jit(solution)/shard_map/ppermute | solution.py:237
  9.0 1.3 collective-permute-start.1
  10.3 0.7 convert_convert_fusion
  11.0 0.7 compare_convert_fusion
  11.7 0.7 stack.43
  12.4 0.8 mul.267
  13.2 1.5 %fusion.9 = (bf16[516,2,1]{2,1,0:T(2,128)(2,1)S(1)}, bf16[516,2,1]{2,1,0:T(2,128)(2,1)S(1)}) fusion(bf16[516,2,512]{2,1,0:T(2,128)(2,1)} %param.28), kind=kLoop, calls=%fused_computation.68 | loop fusion | bytes 8256 | tf_op jit(solution)/shard_map/slice | solution.py:238
  17.2 0.2 copy.107
  17.4 1.0 copy.119.ycol.refs_6_
  19.2 0.2 copy.108
  19.7 0.8 mul.239.mx
  20.5 1.3 or_convert_fusion.refs_7_
  21.8 0.6 pad_maximum_fusion.6.refs_5_
  22.4 0.6 select_maximum_fusion.refs_9_
  23.1 0.6 pad_maximum_fusion.1.refs_8_
  23.7 0.6 concatenate.47.dy
  24.3 0.6 concatenate.46.dx
  25.9 0.8 mul.257.my
  26.7 11.4 %stats.1 = (bf16[10,48,1032]{2,1,0:T(8,128)(2,1)}, bf16[6,48,512]{2,1,0:T(8,128)(2,1)}, f32[8,128]{1,0:T(8,128)}) custom-call(bf16[3,4,1032,512]{3,2,1,0:T(8,128)(2,1)} %vel.3, bf16[8,512]{1,0:T(8,128)(2,1)} %concatenate.46.dx, bf16[8,1032]{1,0:T(8,128)(2,1)} %concatenate.47.dy, f32[160,32]{1,0:T(8,128)} %mul.239.mx, f32[96,32]{1,0:T(8,128)} %mul.257.my, ...), custom_call_target="tpu_custom_call" | custom-call | tf_op jit(solution)/shard_map/stats/pallas_call | solution.py:307
  38.1 25.7 %exchange.1 = (bf16[10,48,1032]{2,1,0:T(8,128)(2,1)}, bf16[6,48,512]{2,1,0:T(8,128)(2,1)}, f32[4,8,8,128]{3,2,1,0:T(8,128)}, bf16[512,1024]{1,0:T(8,128)(2,1)}, ...) custom-call(bf16[10,48,1032]{2,1,0:T(8,128)(2,1)} %get-tuple-element.12.refs_0_, ...), custom_call_target="tpu_custom_call" | custom-call | tf_op jit(solution)/shard_map/exchange/pallas_call | solution.py:334
  63.8 71.2 %sub_step.1 = (bf16[3,4,1032,512]{3,2,1,0:T(8,128)(2,1)}, bf16[3,4,1032,512]{3,2,1,0:T(8,128)(2,1)}) custom-call(bf16[3,4,1032,512]{3,2,1,0:T(8,128)(2,1)} %vel.3, bf16[3,4,1032,512]{3,2,1,0:T(8,128)(2,1)} %prev.1, bf16[10,48,1032]{2,1,0:T(8,128)(2,1)} %get-tuple-element.15.xr, bf16[6,48,512]{2,1,0:T(8,128)(2,1)} %get-tuple-element.16.yr, ...), custom_call_target="tpu_custom_call" | custom-call | tf_op jit(solution)/shard_map/sub_step/pallas_call | solution.py:359
  (90 shorter events, 3.8 us)
Async XLA Ops:
  0.6 14.6 %copy-start.1 = (bf16[516,2,512]{2,1,0:T(2,128)(2,1)S(1)}, bf16[516,2,512]{2,1,0:T(2,128)(2,1)}, u32[]{:S(2)}) copy-start(bf16[516,2,512]{2,1,0:T(2,128)(2,1)} %param.28) | copy-start | bytes 3170308
  0.6 15.6 %copy-start.3 = (f32[512]{0:T(512)S(1)}, f32[512]{0:T(512)}, u32[]{:S(2)}) copy-start(f32[512]{0:T(512)} %param.24) | copy-start | bytes 6148
  0.7 15.6 %copy-start.4 = (f32[1032]{0:T(1024)S(1)}, f32[1032]{0:T(1024)}, u32[]{:S(2)}) copy-start(f32[1032]{0:T(1024)} %param.27) | copy-start | bytes 12388
  0.7 15.6 %copy-start.8 = (f32[2,8,8]{2,1,0:T(8,128)S(1)}, f32[2,8,8]{2,1,0:T(8,128)}, u32[]{:S(2)}) copy-start(f32[2,8,8]{2,1,0:T(8,128)} %param.32) | copy-start | bytes 1540
  0.7 15.7 %copy-start.9 = (f32[2,2,512]{2,1,0:T(2,128)S(1)}, f32[2,2,512]{2,1,0:T(2,128)}, u32[]{:S(2)}) copy-start(f32[2,2,512]{2,1,0:T(2,128)} %param.30) | copy-start | bytes 24580
  3.3 13.6 %copy-start.6 = (f32[2,16,16]{2,1,0:T(8,128)S(1)}, f32[2,16,16]{2,1,0:T(8,128)}, u32[]{:S(2)}) copy-start(f32[2,16,16]{2,1,0:T(8,128)} %param.29) | copy-start | bytes 6148
  4.9 12.1 %copy-start.5 = (f32[1,2,2,1032]{3,2,1,0:T(2,128)S(1)}, f32[1,2,2,1032]{3,2,1,0:T(2,128)}, u32[]{:S(2)}) copy-start(f32[1,2,2,1032]{3,2,1,0:T(2,128)} %param.33) | copy-start | bytes 49540
  5.0 20.0 %collective-permute-start = (bf16[2,2,2]{2,1,0:T(2,128)(2,1)S(1)}, bf16[2,2,2]{2,1,0:T(2,128)(2,1)S(1)}, u32[]{:S(2)}, u32[]{:S(2)}) collective-permute-start(bf16[2,2,2]{2,1,0:T(2,128)(2,1)S(1)} %get-tuple-element.28), channel_id=1, source_target_pairs={{0,8},{8,16},{16,24},{1,9},{9,17},{17,25},{2,10},{10,18},{18,26},{... | collective-permute-start | bytes 56 | tf_op jit(solution)/shard_map/ppermute | solution.py:237
  9.0 16.0 %collective-permute-start.1 = (bf16[2,2,2]{2,1,0:T(2,128)(2,1)S(1)}, bf16[2,2,2]{2,1,0:T(2,128)(2,1)S(1)}, u32[]{:S(2)}, u32[]{:S(2)}) collective-permute-start(bf16[2,2,2]{2,1,0:T(2,128)(2,1)S(1)} %get-tuple-element.29), channel_id=1, source_target_pairs={{8,0},{16,8},{24,16},{9,1},{17,9},{25,17},{10,2},{18,10},{26,18},{... | collective-permute-start | bytes 56 | tf_op jit(solution)/shard_map/ppermute | solution.py:236
  14.7 4.8 %copy-start.12 = (f32[2,4,8]{2,0,1:T(2,128)S(1)}, f32[2,4,8]{2,0,1:T(2,128)}, u32[]{:S(2)}) copy-start(f32[2,4,8]{2,0,1:T(2,128)} %constant.112) | copy-start | bytes 772
  14.7 4.8 %copy-start.7 = (f32[4,4]{1,0:T(4,128)S(1)}, f32[4,4]{1,0:T(4,128)}, u32[]{:S(2)}) copy-start(f32[4,4]{1,0:T(4,128)} %constant.111) | copy-start | bytes 196
  15.3 6.5 %copy-start.10 = (f32[512]{0:T(512)S(1)}, f32[512]{0:T(512)}, u32[]{:S(2)}) copy-start(f32[512]{0:T(512)} %param.25) | copy-start | bytes 6148
  15.3 7.1 %copy-start.2 = (f32[1032]{0:T(1024)S(1)}, f32[1032]{0:T(1024)}, u32[]{:S(2)}) copy-start(f32[1032]{0:T(1024)} %param.26) | copy-start | bytes 12388
  15.3 10.5 %copy-start.11 = (f32[2,4,8]{2,1,0:T(4,128)S(1)}, f32[2,4,8]{2,1,0:T(4,128)}, u32[]{:S(2)}) copy-start(f32[2,4,8]{2,1,0:T(4,128)} %constant.98.clone) | copy-start | bytes 772
  15.5 22.6 %copy-start = (bf16[516,2,512]{2,0,1:T(8,128)(2,1)}, bf16[516,2,512]{2,0,1:T(8,128)(2,1)S(1)}, u32[]{:S(2)}) copy-start(bf16[516,2,512]{2,0,1:T(8,128)(2,1)S(1)} %copy.126) | copy-start | bytes 3170308

commit v3 on v2

--- a/solution.py
+++ b/solution.py
@@ -172,13 +172,16 @@
     if filled < thin.shape[0]:
         thin[filled:, :] = jnp.zeros((thin.shape[0] - filled, width), bf16)
     lines = xr[...].reshape(xr.shape[0] * xr.shape[1], rows)
+    across = jnp.concatenate([lx[...], bx[0]], axis=0)
+    along = jnp.concatenate([vel[f, 0, 0:main, :], thin[...]], axis=0)
     starts = list(range(0, main, tile))
     for start in starts:
         stop = rows if start == starts[-1] else start + tile
         here = slice(start, stop)
-        ax = dot(vel[f, 0, here, :], lx[...]) + dot(lines[:, here], bx[0], 0, 0)
-        ay0 = dot(wy[0, here, :], vel[f, 0, 0:main, :]) + dot(wt[0, 0, here, :], thin[...])
-        ay1 = dot(wy[1, here, :], vel[f, 0, 0:main, :]) + dot(wt[0, 1, here, :], thin[...])
+        points = jnp.concatenate([vel[f, 0, here, :], lines[:, here].T], axis=1)
+        ax = dot(points, across)
+        ay0 = dot(jnp.concatenate([wy[0, here, :], wt[0, 0, here, :]], axis=1), along)
+        ay1 = dot(jnp.concatenate([wy[1, here, :], wt[0, 1, here, :]], axis=1), along)
         u = vel[0, 0, here, :].astype(f32)
         v = vel[1, 0, here, :].astype(f32)
         live = ycol[here, 1:2] > 0.0

time: 136 us -> 134 us (0.985)
  Pallas kernels: 108 us -> 106 us
    pallas_call x1, Pallas kernels: 71.2 us -> 69.1 us  [shards(): pl.pallas_call(functools.partial(main_kernel, main, tile), name='sub_step...]
where the time goes in v3:
time: 134 us; the launch traced here: 133 us
  Pallas kernels  106 us (79%)
  local copies, waits for them, and re-layouts  12 us (9%)
  other arithmetic  6.36 us (5%)
  starting transfers between devices  5.3 us (4%)
  between operations  3.04 us (2%)
    pallas_call x1, Pallas kernels, shards(): pl.pallas_call(functools.partial(main_kernel, main, tile), name='sub_step...  69.1 us
    pallas_call x1, Pallas kernels, shards(): pl.pallas_call(functools.partial(exchange_kernel, n_row, n_col), name='ex...  25.7 us
    pallas_call x1, Pallas kernels, shards(): pl.pallas_call(stats_kernel, name='stats', grid=(n_plane,), in_specs=[fie...  11.4 us
    ppermute x1, starting transfers between devices, shards(): prior_y = lax.ppermute(y_ends[:, :, rows + 2:], 'row', up).astype(f32)  4.01 us
  transfers between devices with their start and end apart: 2, of which 0 were waited for; matrix products, arithmetic and copies ran while one was open for 10% of the time, Pallas kernels for 0%

profile of v3, /device:TPU:1, one launch (start us, length us, event | category | flops | bytes accessed | tf_op | source)
XLA Modules:
  0.0 133.0 jit_solution(15848477415378265330)
XLA Ops:
  0.7 1.3 dynamic_slice.27
  3.3 0.8 dynamic-slice_bitcast_fusion
  4.1 0.8 slice.72
  5.0 4.0 %collective-permute-start = (bf16[2,2,2]{2,1,0:T(2,128)(2,1)S(1)}, bf16[2,2,2]{2,1,0:T(2,128)(2,1)S(1)}, u32[]{:S(2)}, u32[]{:S(2)}) collective-permute-start(bf16[2,2,2]{2,1,0:T(2,128)(2,1)S(1)} %get-tuple-element.28), channel_id=1, source_target_pairs={{0,8},{8,16},{16,24},{1,9},{9,17},{17,25},{2,10},{10,18},{18,26},{... | collective-permute-start | bytes 56 | tf_op jit(solution)/shard_map/ppermute | solution.py:240
  9.0 1.3 collective-permute-start.1
  10.3 0.7 convert_convert_fusion
  11.0 0.7 compare_convert_fusion
  11.7 0.7 stack.43
  12.4 0.8 mul.267
  13.2 1.5 %fusion.9 = (bf16[516,2,1]{2,1,0:T(2,128)(2,1)S(1)}, bf16[516,2,1]{2,1,0:T(2,128)(2,1)S(1)}) fusion(bf16[516,2,512]{2,1,0:T(2,128)(2,1)} %param.28), kind=kLoop, calls=%fused_computation.68 | loop fusion | bytes 8256 | tf_op jit(solution)/shard_map/slice | solution.py:241
  17.2 0.2 copy.107
  17.4 1.0 copy.119.ycol.refs_6_
  19.2 0.2 copy.108
  19.7 0.8 mul.239.mx
  20.5 1.3 or_convert_fusion.refs_7_
  21.8 0.6 pad_maximum_fusion.6.refs_5_
  22.4 0.6 select_maximum_fusion.refs_9_
  23.1 0.6 pad_maximum_fusion.1.refs_8_
  23.7 0.6 concatenate.47.dy
  24.3 0.6 concatenate.46.dx
  25.9 0.8 mul.257.my
  26.7 11.4 %stats.1 = (bf16[10,48,1032]{2,1,0:T(8,128)(2,1)}, bf16[6,48,512]{2,1,0:T(8,128)(2,1)}, f32[8,128]{1,0:T(8,128)}) custom-call(bf16[3,4,1032,512]{3,2,1,0:T(8,128)(2,1)} %vel.3, bf16[8,512]{1,0:T(8,128)(2,1)} %concatenate.46.dx, bf16[8,1032]{1,0:T(8,128)(2,1)} %concatenate.47.dy, f32[160,32]{1,0:T(8,128)} %mul.239.mx, f32[96,32]{1,0:T(8,128)} %mul.257.my, ...), custom_call_target="tpu_custom_call" | custom-call | tf_op jit(solution)/shard_map/stats/pallas_call | solution.py:310
  38.1 25.7 %exchange.1 = (bf16[10,48,1032]{2,1,0:T(8,128)(2,1)}, bf16[6,48,512]{2,1,0:T(8,128)(2,1)}, f32[4,8,8,128]{3,2,1,0:T(8,128)}, bf16[512,1024]{1,0:T(8,128)(2,1)}, ...) custom-call(bf16[10,48,1032]{2,1,0:T(8,128)(2,1)} %get-tuple-element.12.refs_0_, ...), custom_call_target="tpu_custom_call" | custom-call | tf_op jit(solution)/shard_map/exchange/pallas_call | solution.py:337
  63.8 69.1 %sub_step.1 = (bf16[3,4,1032,512]{3,2,1,0:T(8,128)(2,1)}, bf16[3,4,1032,512]{3,2,1,0:T(8,128)(2,1)}) custom-call(bf16[3,4,1032,512]{3,2,1,0:T(8,128)(2,1)} %vel.3, bf16[3,4,1032,512]{3,2,1,0:T(8,128)(2,1)} %prev.1, bf16[10,48,1032]{2,1,0:T(8,128)(2,1)} %get-tuple-element.15.xr, bf16[6,48,512]{2,1,0:T(8,128)(2,1)} %get-tuple-element.16.yr, ...), custom_call_target="tpu_custom_call" | custom-call | tf_op jit(solution)/shard_map/sub_step/pallas_call | solution.py:362
  (90 shorter events, 3.8 us)
Async XLA Ops:
  0.6 14.6 %copy-start.1 = (bf16[516,2,512]{2,1,0:T(2,128)(2,1)S(1)}, bf16[516,2,512]{2,1,0:T(2,128)(2,1)}, u32[]{:S(2)}) copy-start(bf16[516,2,512]{2,1,0:T(2,128)(2,1)} %param.28) | copy-start | bytes 3170308
  0.6 15.6 %copy-start.3 = (f32[512]{0:T(512)S(1)}, f32[512]{0:T(512)}, u32[]{:S(2)}) copy-start(f32[512]{0:T(512)} %param.24) | copy-start | bytes 6148
  0.7 15.6 %copy-start.4 = (f32[1032]{0:T(1024)S(1)}, f32[1032]{0:T(1024)}, u32[]{:S(2)}) copy-start(f32[1032]{0:T(1024)} %param.27) | copy-start | bytes 12388
  0.7 15.6 %copy-start.8 = (f32[2,8,8]{2,1,0:T(8,128)S(1)}, f32[2,8,8]{2,1,0:T(8,128)}, u32[]{:S(2)}) copy-start(f32[2,8,8]{2,1,0:T(8,128)} %param.32) | copy-start | bytes 1540
  0.7 15.7 %copy-start.9 = (f32[2,2,512]{2,1,0:T(2,128)S(1)}, f32[2,2,512]{2,1,0:T(2,128)}, u32[]{:S(2)}) copy-start(f32[2,2,512]{2,1,0:T(2,128)} %param.30) | copy-start | bytes 24580
  3.3 13.6 %copy-start.6 = (f32[2,16,16]{2,1,0:T(8,128)S(1)}, f32[2,16,16]{2,1,0:T(8,128)}, u32[]{:S(2)}) copy-start(f32[2,16,16]{2,1,0:T(8,128)} %param.29) | copy-start | bytes 6148
  4.9 12.1 %copy-start.5 = (f32[1,2,2,1032]{3,2,1,0:T(2,128)S(1)}, f32[1,2,2,1032]{3,2,1,0:T(2,128)}, u32[]{:S(2)}) copy-start(f32[1,2,2,1032]{3,2,1,0:T(2,128)} %param.33) | copy-start | bytes 49540
  5.0 20.0 %collective-permute-start = (bf16[2,2,2]{2,1,0:T(2,128)(2,1)S(1)}, bf16[2,2,2]{2,1,0:T(2,128)(2,1)S(1)}, u32[]{:S(2)}, u32[]{:S(2)}) collective-permute-start(bf16[2,2,2]{2,1,0:T(2,128)(2,1)S(1)} %get-tuple-element.28), channel_id=1, source_target_pairs={{0,8},{8,16},{16,24},{1,9},{9,17},{17,25},{2,10},{10,18},{18,26},{... | collective-permute-start | bytes 56 | tf_op jit(solution)/shard_map/ppermute | solution.py:240
  9.0 16.0 %collective-permute-start.1 = (bf16[2,2,2]{2,1,0:T(2,128)(2,1)S(1)}, bf16[2,2,2]{2,1,0:T(2,128)(2,1)S(1)}, u32[]{:S(2)}, u32[]{:S(2)}) collective-permute-start(bf16[2,2,2]{2,1,0:T(2,128)(2,1)S(1)} %get-tuple-element.29), channel_id=1, source_target_pairs={{8,0},{16,8},{24,16},{9,1},{17,9},{25,17},{10,2},{18,10},{26,18},{... | collective-permute-start | bytes 56 | tf_op jit(solution)/shard_map/ppermute | solution.py:239
  14.7 4.8 %copy-start.12 = (f32[2,4,8]{2,0,1:T(2,128)S(1)}, f32[2,4,8]{2,0,1:T(2,128)}, u32[]{:S(2)}) copy-start(f32[2,4,8]{2,0,1:T(2,128)} %constant.112) | copy-start | bytes 772
  14.7 4.8 %copy-start.7 = (f32[4,4]{1,0:T(4,128)S(1)}, f32[4,4]{1,0:T(4,128)}, u32[]{:S(2)}) copy-start(f32[4,4]{1,0:T(4,128)} %constant.111) | copy-start | bytes 196
  15.3 6.5 %copy-start.10 = (f32[512]{0:T(512)S(1)}, f32[512]{0:T(512)}, u32[]{:S(2)}) copy-start(f32[512]{0:T(512)} %param.25) | copy-start | bytes 6148
  15.3 7.1 %copy-start.2 = (f32[1032]{0:T(1024)S(1)}, f32[1032]{0:T(1024)}, u32[]{:S(2)}) copy-start(f32[1032]{0:T(1024)} %param.26) | copy-start | bytes 12388
  15.3 10.5 %copy-start.11 = (f32[2,4,8]{2,1,0:T(4,128)S(1)}, f32[2,4,8]{2,1,0:T(4,128)}, u32[]{:S(2)}) copy-start(f32[2,4,8]{2,1,0:T(4,128)} %constant.98.clone) | copy-start | bytes 772
  15.5 22.6 %copy-start = (bf16[516,2,512]{2,0,1:T(8,128)(2,1)}, bf16[516,2,512]{2,0,1:T(8,128)(2,1)S(1)}, u32[]{:S(2)}) copy-start(bf16[516,2,512]{2,0,1:T(8,128)(2,1)S(1)} %copy.126) | copy-start | bytes 3170308
